TPU v7x, 512 devices: a whole 4x8x8 slice. The times are simulated.
512 devices in a mesh: elem: 32 (over z, y_lo), mode: 16 (over x, y_hi, core).
Axes of the slice: x: 4, y: 8 (y_hi: 2, y_lo: 4; y = y_hi * 4 + y_lo), z: 8, core: 2. Of those that a mesh axis runs over, the one named last changes fastest.
Arguments:
- modal_history: float32 [4096, 512], P('elem', 'mode'), may hold values from -6 to 6
- stress_modes: float32 [512, 6144], P('mode', 'elem'), may hold values from -0.5 to 0.5
Outputs:
- stress_spectrum: float32 [6144, 2, 2048], P(('elem', 'mode'))
All inputs are finite; a program needn't handle non-finite values.
Results may differ from a plain program's by a relative error of at most 0.00007.
Values sent between devices are 32-bit elements; how exact they have to be, the bound alone decides.
No kernel may reach another device: no remote copies, remote signals or barrier semaphores. Data moves between devices by JAX's collectives and lax.ppermute only.
A program may use at most 64 MiB of HBM per device.

v0:
```python
import math

import jax
import jax.numpy as jnp
from jax import lax
from jax.sharding import PartitionSpec as P

highest = lax.Precision.HIGHEST


def spectra(signal):
    columns = signal.shape[0]
    radix = 64
    halved = radix // 2
    blocked = signal.reshape(columns, radix, radix)
    counter = jnp.arange(radix, dtype=jnp.int32)
    products = counter[:, None] * counter[None, :]
    small_angle = (products % radix).astype(jnp.float32) * (2.0 * math.pi / radix)
    cosine_small = jnp.cos(small_angle)
    sine_small = jnp.sin(small_angle)
    twist_angle = (products % (radix * radix)).astype(jnp.float32) * (
        2.0 * math.pi / (radix * radix)
    )
    twist_cos = jnp.cos(twist_angle)
    twist_sin = jnp.sin(twist_angle)
    first_real = jnp.einsum("cab,ak->cbk", blocked, cosine_small, precision=highest)
    first_imag = -jnp.einsum("cab,ak->cbk", blocked, sine_small, precision=highest)
    turned_real = first_real * twist_cos + first_imag * twist_sin
    turned_imag = first_imag * twist_cos - first_real * twist_sin
    cosine_half = cosine_small[:, :halved]
    sine_half = sine_small[:, :halved]
    final_real = jnp.einsum(
        "cbk,bj->cjk", turned_real, cosine_half, precision=highest
    ) + jnp.einsum("cbk,bj->cjk", turned_imag, sine_half, precision=highest)
    final_imag = jnp.einsum(
        "cbk,bj->cjk", turned_imag, cosine_half, precision=highest
    ) - jnp.einsum("cbk,bj->cjk", turned_real, sine_half, precision=highest)
    stacked = jnp.stack([final_real, final_imag], axis=1) * (1.0 / radix)
    return stacked.reshape(columns, 2, halved * radix)


def per_device(modal_history, stress_modes):
    elem_count = lax.axis_size("elem")
    mode_count = lax.axis_size("mode")
    local_steps = modal_history.shape[0]
    partial_value = jnp.einsum(
        "mp,tm->pt",
        lax.all_gather(stress_modes, "elem", axis=1, tiled=True),
        modal_history,
        precision=highest,
        preferred_element_type=jnp.float32,
    )
    owned_width = partial_value.shape[0] // (elem_count * mode_count)
    reordered = partial_value.reshape(elem_count, mode_count, owned_width, local_steps)
    reordered = reordered.transpose(1, 0, 2, 3).reshape(
        mode_count * elem_count * owned_width, local_steps
    )
    summed = lax.psum_scatter(reordered, "mode", scatter_dimension=0, tiled=True)
    stress = lax.all_to_all(summed, "elem", split_axis=0, concat_axis=1, tiled=True)
    return spectra(stress)


def solution(mesh):
    placed = (P("elem", "mode"), P("mode", "elem"))
    return jax.shard_map(
        per_device,
        mesh=mesh,
        in_specs=placed,
        out_specs=P(("elem", "mode"), None, None),
        check_vma=False,
    )
```

profile of v0, /device:TPU:1, one launch (start us, length us, event | category | flops | bytes accessed | tf_op | source)
XLA Modules:
  0.0 249.4 jit_solution(8755520814195808711)
XLA Ops:
  6.5 0.0 copy-start
  6.5 0.0 reduce-scatter.2.cloned.1.call-start
  6.5 82.1 %all-gather = f32[32,192,32]{1,2,0:T(8,128)S(1)} all-gather(f32[1,192,32]{1,2,0:T(8,128)} %bitcast.31), channel_id=1, replica_groups=mesh['elem'=32,'mode'=16] {'elem'}, dimensions={0}, use_global_device_ids=true | all-gather | bytes 811008 | tf_op jit(solution)/shard_map/all_gather | solution.py:48
  88.6 0.6 copy.19
  89.2 1.3 reshape.58
  90.5 0.0 copy-done
  90.5 6.2 %fusion.32 = f32[6144,128]{1,0:T(8,128)S(1)} fusion(f32[6144,32]{0,1:T(8,128)} %reshape.58, f32[128,32]{0,1:T(8,128)S(1)} %copy-done), kind=kOutput, calls=%fused_computation.44 | convolution fusion | flops 301989888 | bytes 3948544 | tf_op jit(solution)/shard_map/mp,tm->pt/dot_general | solution.py:46
  96.7 2.1 reshape.54
  98.8 4.6 %copy.20 = f32[16,32,12,128]{3,2,1,0:T(8,128)} copy(f32[16,32,12,128]{3,2,0,1:T(8,128)} %bitcast.29) | data formatting | bytes 6291456 | tf_op jit(solution)/shard_map/transpose | solution.py:55
  103.4 4.6 %reshape.55 = f32[6144,128]{1,0:T(8,128)} reshape(f32[16,32,12,128]{3,2,1,0:T(8,128)} %copy.20) | data formatting | bytes 6291456 | tf_op jit(solution)/shard_map/reshape | solution.py:55
  108.0 0.0 reduce-scatter.2.cloned.1.call-update
  108.0 109.4 %reduce-scatter.2.cloned.1.call-done = f32[384,128]{1,0:T(8,128)} async-done(((f32[6144,128]{1,0:T(8,128)}), f32[384,128]{1,0:T(8,128)}) %reduce-scatter.2.cloned.1.call-update) | async-done | bytes 196624 | tf_op jit(solution)/shard_map/reduce_scatter | solution.py:58
  217.5 1.6 all_to_all.12
  219.1 8.3 %all-to-all-start = ((f32[32,12,128]{2,1,0:T(8,128)}), f32[32,12,128]{2,1,0:T(8,128)S(1)}, u32[]{:S(2)}, u32[]{:S(2)}) async-start(f32[32,12,128]{2,1,0:T(8,128)} %all_to_all.12), calls=%async_computation.1 | async-start | bytes 524288 | tf_op jit(solution)/shard_map/all_to_all | solution.py:59
  227.4 0.1 fusion.19
  227.5 0.1 copy.24
  227.6 0.1 fusion.18
  227.8 0.1 copy.27
  227.8 0.2 fusion.21
  228.0 0.1 fusion.20
  228.1 10.1 %all-to-all-done = f32[32,12,128]{2,1,0:T(8,128)S(1)} async-done(((f32[32,12,128]{2,1,0:T(8,128)}), f32[32,12,128]{2,1,0:T(8,128)S(1)}, u32[]{:S(2)}, u32[]{:S(2)}) %all-to-all-start) | async-done | bytes 196640 | tf_op jit(solution)/shard_map/all_to_all | solution.py:59
  238.2 0.1 copy.21
  238.3 0.1 reshape.56
  238.4 0.8 convolution_negate_fusion
  239.2 0.8 fusion.9
  240.1 0.4 fusion.2
  240.4 0.4 fusion.3
  240.8 0.4 fusion.1
  241.2 0.1 stack.9
  241.3 0.4 fusion
  241.6 0.1 stack.10
  241.8 0.8 copy.28
  (1 shorter events, 0.0 us)
Async XLA Ops:
  6.5 84.0 %copy-start = (f32[128,32]{0,1:T(8,128)S(1)}, f32[128,32]{0,1:T(8,128)}, u32[]{:S(2)}) copy-start(f32[128,32]{0,1:T(8,128)} %param.2) | copy-start | bytes 49156
  6.5 210.9 %reduce-scatter.2.cloned.1.call-start = ((), (), s32[]{:S(2)}) async-start(), calls=%async_computation.2 | async-start | bytes 3342336 | tf_op jit(solution)/shard_map/reduce_scatter | solution.py:58
  219.1 19.1 %all-to-all-start = ((f32[32,12,128]{2,1,0:T(8,128)}), f32[32,12,128]{2,1,0:T(8,128)S(1)}, u32[]{:S(2)}, u32[]{:S(2)}) async-start(f32[32,12,128]{2,1,0:T(8,128)} %all_to_all.12), calls=%async_computation.1 | async-start | bytes 524288 | tf_op jit(solution)/shard_map/all_to_all | solution.py:59
Sparse Core Ops, SparseCore 0:
  108.1 109.2 reduce-scatter.1
where the time goes:
time: 251 us; the launch traced here: 249 us
  waiting for transfers between devices  120 us (48%)
  blocking collectives  82.1 us (33%)
  local copies, waits for them, and re-layouts  16.2 us (6%)
  between operations  13.5 us (5%)
  matrix products  9.24 us (4%)
  starting transfers between devices  8.29 us (3%)
    reduce_scatter x1, waiting for transfers between devices, per_device(): lax.psum_scatter(reordered, 'mode', scatter_dimension=0, tiled=True)  109 us
    all_gather x1, blocking collectives, per_device(): lax.all_gather(stress_modes, 'elem', axis=1, tiled=True)  82.1 us
    all_to_all x1, waiting for transfers between devices, per_device(): lax.all_to_all(summed, 'elem', split_axis=0, concat_axis=1, tiled=True)  10.1 us
    all_to_all x1, starting transfers between devices, per_device(): lax.all_to_all(summed, 'elem', split_axis=0, concat_axis=1, tiled=True)  8.28 us
    dot_general x1, matrix products, per_device(): jnp.einsum('mp,tm->pt', lax.all_gather(stress_modes, 'elem', axis=1, tile...  6.19 us
  transfers between devices with their start and end apart: 2, of which 2 were waited for; matrix products, arithmetic and copies ran while one was open for 0% of the time, Pallas kernels for 0%

commit v1 on v0

v1 whole, which is shorter than its diff:
```python
import numpy as np

import jax
import jax.numpy as jnp
from jax import lax
from jax.sharding import Mesh, PartitionSpec as P

highest = lax.Precision.HIGHEST

PARTS = ("z", "yl", "x", "yh", "c")
SIZES = (8, 4, 4, 2, 2)
ELEM = ("z", "yl")
MODE = ("x", "yh", "c")
PAIR = ("x", "c")
STEPS = 4096
SLOW, FAST = 128, 32


def tables():
    k1 = np.arange(SLOW)
    n1 = np.arange(SLOW)
    angle = 2.0 * np.pi * ((n1[:, None] * k1[None, :]) % SLOW) / SLOW
    eye = np.eye(4)
    first = np.stack([np.cos(angle), -np.sin(angle)], axis=1)
    first = np.einsum("npk,bc->nbcpk", first, eye).reshape(4 * SLOW, 4 * 2 * SLOW)
    n2 = np.arange(FAST)
    turn = 2.0 * np.pi * (n2[:, None] * k1[None, :]) / STEPS
    twist = np.stack([np.cos(turn), -np.sin(turn)])
    k2 = np.arange(FAST // 2)
    angle = 2.0 * np.pi * ((n2[:, None] * k2[None, :]) % FAST) / FAST
    real, imag = np.cos(angle) / 64.0, -np.sin(angle) / 64.0
    last = np.stack([np.stack([real, -imag]), np.stack([imag, real])])
    return [np.asarray(a, np.float32) for a in (first, twist, last)]


def spectra(gathered):
    first, twist, last = tables()
    summed = gathered[:, 0] + gathered[:, 1]
    columns = summed.shape[2]
    rows = summed.reshape(8 * columns, 4 * SLOW)
    stage = jnp.dot(rows, first, precision=highest).reshape(8, columns, 4, 2, SLOW)
    stage = stage.transpose(3, 1, 0, 2, 4).reshape(2, columns, FAST, SLOW)
    turned = jnp.stack(
        [
            stage[0] * twist[0] - stage[1] * twist[1],
            stage[0] * twist[1] + stage[1] * twist[0],
        ]
    )
    out = jnp.einsum("oink,icna->coka", last, turned, precision=highest)
    return out.reshape(columns, 2, STEPS // 2)


def per_device(modal_history, stress_modes):
    local_modes, width = stress_modes.shape
    pieces = modal_history.T.reshape(local_modes, 4, 8, 4).transpose(2, 0, 1, 3)
    pieces = pieces.reshape(8, local_modes, 16)
    sent = jnp.concatenate(
        [jnp.broadcast_to(stress_modes, (8, local_modes, width)), pieces], axis=2
    )
    got = lax.all_to_all(sent, PAIR, split_axis=0, concat_axis=0, tiled=True)
    modes = got[:, :, :width].reshape(8 * local_modes, width)
    history = got[:, :, width:].reshape(8 * local_modes, 16).T
    spread = jnp.broadcast_to(history, (32,) + history.shape)
    steps = lax.all_to_all(spread, ELEM, split_axis=0, concat_axis=0, tiled=True)
    steps = steps.reshape(32 * 16, 8 * local_modes)
    partial = jnp.einsum("mp,tm->pt", modes, steps, precision=highest)
    partial = partial.reshape(16, width // 16, 32 * 16)
    owned = lax.all_to_all(partial, MODE, split_axis=0, concat_axis=0, tiled=True)
    return spectra(owned.reshape(4, 2, 2, width // 16, 32 * 16))


def solution(mesh):
    parts = Mesh(mesh.devices.reshape(SIZES), PARTS)
    return jax.shard_map(
        per_device,
        mesh=parts,
        in_specs=(P(ELEM, MODE), P(MODE, ELEM)),
        out_specs=P(PARTS, None, None),
        check_vma=False,
    )
```

time: 251 us -> 75 us (0.30)
  the two profiles are of different devices: /device:TPU:1 before, /device:TPU:8 now
where the time goes in v1:
time: 75 us; the launch traced here: 74.6 us
  blocking collectives  36.9 us (49%)
  waiting for transfers between devices  16.4 us (22%)
  starting transfers between devices  14 us (19%)
  local copies, waits for them, and re-layouts  3.7 us (5%)
  matrix products  3.27 us (4%)
    all_to_all x1, blocking collectives, per_device(): lax.all_to_all(partial, MODE, split_axis=0, concat_axis=0, tiled=True)  25.3 us
    all_to_all x1, waiting for transfers between devices, per_device(): lax.all_to_all(spread, ELEM, split_axis=0, concat_axis=0, tiled=True)  16.4 us
    all_to_all x1, starting transfers between devices, per_device(): lax.all_to_all(spread, ELEM, split_axis=0, concat_axis=0, tiled=True)  14 us
    all_to_all x1, blocking collectives, per_device(): got = lax.all_to_all(sent, PAIR, split_axis=0, concat_axis=0, tiled=True)  11.6 us
    dot_general x1, matrix products, spectra(): jnp.dot(rows, first, precision=highest).reshape(8, columns, 4, 2, SLOW)  2.28 us
  transfers between devices with their start and end apart: 1, of which 1 were waited for; matrix products, arithmetic and copies ran while one was open for 0% of the time, Pallas kernels for 0%

profile of v1, /device:TPU:8, one launch (start us, length us, event | category | flops | bytes accessed | tf_op | source)
XLA Modules:
  0.0 74.6 jit_solution(3585747007009914223)
XLA Ops:
  0.0 0.8 %copy.26 = f32[128,32]{1,0:T(8,128)S(1)} copy(f32[128,32]{0,1:T(8,128)} %param.8) | data formatting | bytes 32768 | tf_op args[0]
  0.8 0.1 copy.28
  0.9 0.8 %broadcast_in_dim.4 = f32[8,32,192]{2,1,0:T(8,128)S(1)} broadcast(f32[32,192]{1,0:T(8,128)} %param.9), dimensions={1,2} | broadcast | bytes 221184 | tf_op jit(solution)/shard_map/broadcast_in_dim | solution.py:58
  1.7 0.1 pad_maximum_fusion
  1.8 11.6 %all_to_all.15 = f32[8,32,208]{2,1,0:T(8,128)S(1)} all-to-all(f32[8,32,208]{2,1,0:T(8,128)S(1)} %pad_maximum_fusion), channel_id=1, replica_groups=mesh['z'=8,'yl'=4,'x'=4,'yh'=2,'c'=2] {'x','c'}, dimensions={0} | all-to-all | bytes 425984 | tf_op jit(solution)/shard_map/all_to_all | solution.py:60
  13.5 0.1 slice.29
  13.6 0.1 copy.30
  13.6 0.9 %broadcast_in_dim.5 = f32[32,16,256]{2,1,0:T(8,128)} broadcast(f32[16,256]{1,0:T(8,128)S(1)} %copy.30), dimensions={1,2} | broadcast | bytes 540672 | tf_op jit(solution)/shard_map/broadcast_in_dim | solution.py:63
  14.5 14.0 %all-to-all-start.1 = ((f32[32,16,256]{2,1,0:T(8,128)}), f32[32,16,256]{2,1,0:T(8,128)S(1)}, u32[]{:S(2)}, u32[]{:S(2)}) async-start(f32[32,16,256]{2,1,0:T(8,128)} %broadcast_in_dim.5), calls=%async_computation.1 | async-start | bytes 1048576 | tf_op jit(solution)/shard_map/all_to_all | solution.py:64
  28.5 0.0 copy-start
  28.5 0.1 copy.29
  28.6 16.4 %all-to-all-done.1 = f32[32,16,256]{2,1,0:T(8,128)S(1)} async-done(((f32[32,16,256]{2,1,0:T(8,128)}), f32[32,16,256]{2,1,0:T(8,128)S(1)}, u32[]{:S(2)}, u32[]{:S(2)}) %all-to-all-start.1) | async-done | bytes 524320 | tf_op jit(solution)/shard_map/all_to_all | solution.py:64
  45.0 0.6 fusion.4
  45.6 25.3 %all_to_all.16 = f32[16,12,512]{2,1,0:T(8,128)S(1)} all-to-all(f32[16,12,512]{2,1,0:T(8,128)S(1)} %fusion.4), channel_id=1, replica_groups=mesh['z'=8,'yl'=4,'x'=4,'yh'=2,'c'=2] {'x','yh','c'}, dimensions={0} | all-to-all | bytes 786432 | tf_op jit(solution)/shard_map/all_to_all | solution.py:68
  70.9 0.0 copy-start.2
  71.0 0.0 copy-start.3
  71.0 0.0 copy-done
  71.0 0.0 copy-start.1
  71.0 2.3 %convolution_bitcast_fusion = f32[2,12,8,4,128]{4,1,0,3,2:T(8,128)S(1)} fusion(f32[8,12,512,1,1]{2,1,4,3,0:T(8,128)S(1)} %bitcast.50, f32[4,2,128,512,1]{3,2,1,0,4:T(8,128)S(1)} %copy-done), kind=kOutput, calls=%fused_computation | convolution fusion | flops 603979776 | bytes 2686976 | tf_op jit(solution)/shard_map/dot_general | solution.py:41
  73.3 0.0 copy-done.2
  73.3 0.0 copy-done.3
  73.4 0.1 multiply_subtract_fusion
  73.5 0.0 copy-done.1
  73.5 0.4 convolution_bitcast_fusion.1
  73.9 0.8 %reshape.93 = f32[12,2,2048]{2,1,0:T(2,128)} reshape(f32[12,2,16,128]{3,2,1,0:T(8,128)S(1)} %convolution_bitcast_fusion.1) | data formatting | bytes 393216 | tf_op jit(solution)/shard_map/reshape | solution.py:50
  (4 shorter events, 0.1 us)
Async XLA Ops:
  14.5 30.5 %all-to-all-start.1 = ((f32[32,16,256]{2,1,0:T(8,128)}), f32[32,16,256]{2,1,0:T(8,128)S(1)}, u32[]{:S(2)}, u32[]{:S(2)}) async-start(f32[32,16,256]{2,1,0:T(8,128)} %broadcast_in_dim.5), calls=%async_computation.1 | async-start | bytes 1048576 | tf_op jit(solution)/shard_map/all_to_all | solution.py:64
  28.5 42.5 %copy-start = (f32[4,2,128,512,1]{3,2,1,0,4:T(8,128)S(1)}, f32[4,2,128,512,1]{3,2,1,0,4:T(8,128)}, u32[]{:S(2)}) copy-start(f32[4,2,128,512,1]{3,2,1,0,4:T(8,128)} %constant.14) | copy-start | bytes 6291460
  70.9 2.4 %copy-start.2 = (f32[32,128]{1,0:T(8,128)S(1)}, f32[32,128]{1,0:T(8,128)}, u32[]{:S(2)}) copy-start(f32[32,128]{1,0:T(8,128)} %constant.10.clone) | copy-start | bytes 49156
  71.0 2.4 %copy-start.3 = (f32[32,128]{1,0:T(8,128)S(1)}, f32[32,128]{1,0:T(8,128)}, u32[]{:S(2)}) copy-start(f32[32,128]{1,0:T(8,128)} %constant.9.clone) | copy-start | bytes 49156
  71.0 2.5 %copy-start.1 = (f32[2,2,32,16,1]{2,3,1,0,4:T(8,128)S(1)}, f32[2,2,32,16,1]{2,3,1,0,4:T(8,128)}, u32[]{:S(2)}) copy-start(f32[2,2,32,16,1]{2,3,1,0,4:T(8,128)} %constant.15) | copy-start | bytes 24580

commit v2 on v1

v2 whole, which is shorter than its diff:
```python
import numpy as np

import jax
import jax.numpy as jnp
from jax import lax
from jax.experimental import pallas as pl
from jax.experimental.pallas import tpu as pltpu
from jax.sharding import Mesh, PartitionSpec as P

PARTS = ("z", "yl", "x", "yh", "c")
SIZES = (8, 4, 4, 2, 2)
ELEM = ("z", "yl")
MODE = ("x", "yh", "c")
BLOCKS, SHARES = 32, 16
STEPS, MODES = 4096, 512
SLOW, FAST = 256, 16
OWNED, PADDED = 12, 16
LANES = 128
f32, bf16 = jnp.float32, jnp.bfloat16
NN = (((1,), (0,)), ((), ()))
NT = (((1,), (1,)), ((), ()))


def split(x):
    high = x.astype(bf16)
    return high, (x - high.astype(f32)).astype(bf16)


def product(a, b, dims):
    (ah, al), (bh, bl) = a, b
    dot = lambda x, y: lax.dot_general(x, y, dims, preferred_element_type=f32)
    return dot(ah, bh) + (dot(ah, bl) + dot(al, bh))


def tables():
    k1 = np.arange(SLOW)
    angle = 2.0 * np.pi * ((k1[:, None] * k1[None, :]) % SLOW) / SLOW
    first = np.concatenate([np.cos(angle), -np.sin(angle)], axis=1) / np.sqrt(STEPS)
    high = first.astype(np.float32).astype(jnp.bfloat16)
    low = (first - high.astype(np.float64)).astype(jnp.bfloat16)
    turn = 2.0 * np.pi * (np.arange(FAST)[:, None] * k1[None, :]) / STEPS
    twist = np.stack([np.cos(turn), -np.sin(turn)])
    return high, low, twist.astype(np.float32)


def share():
    return lax.axis_index(MODE)


def scatter_steps(history_ref, out_ref, wide, tall):
    modes = history_ref.shape[0]
    wide[...] = jnp.zeros_like(wide)
    at = pl.multiple_of(lax.rem(share(), LANES // modes) * modes, modes)
    wide[pl.ds(at, modes), :] = history_ref[...]
    tall[...] = wide[...].T
    for n2 in range(FAST):
        out_ref[n2] = tall[pl.ds(n2, LANES // FAST, stride=FAST), :]


def join_shares(got_ref, out_ref):
    for quad in range(4):
        joined = (got_ref[4 * quad] + got_ref[4 * quad + 1]) + (
            got_ref[4 * quad + 2] + got_ref[4 * quad + 3]
        )
        lanes = pl.ds(quad * LANES, LANES)
        out_ref[:, :, lanes] = jnp.broadcast_to(joined, (BLOCKS,) + joined.shape)


def order_modes(own_ref, one_ref, two_ref, three_ref, high_ref, low_ref, whole):
    x, y, c = lax.axis_index("x"), lax.axis_index("yh"), lax.axis_index("c")
    rows = own_ref.shape[0] // 4
    for shift, ref in enumerate((own_ref, one_ref, two_ref, three_ref)):
        at_x = lax.rem(x + 4 - shift, 4)
        for part in range(4):
            at_y = lax.rem(y + part % 2, 2)
            at_c = lax.rem(c + part // 2, 2)
            at = pl.multiple_of((at_x * 4 + at_y * 2 + at_c) * rows, rows)
            whole[pl.ds(at, rows), :] = ref[pl.ds(part * rows, rows), :]
    high_ref[...], low_ref[...] = split(whole[...].T)


def contract(high_ref, low_ref, steps_ref, out_ref):
    steps = steps_ref[...].reshape(SLOW, MODES)
    stress = product((high_ref[...], low_ref[...]), split(steps), NT)
    for owner in range(SHARES):
        out_ref[owner] = stress[owner * OWNED : (owner + 1) * OWNED, :]


def plus(a, b):
    return a[0] + b[0], a[1] + b[1]


def minus(a, b):
    return a[0] - b[0], a[1] - b[1]


def by_minus_i(a):
    return a[1], -a[0]


def times(a, real, imag):
    return a[0] * real - a[1] * imag, a[0] * imag + a[1] * real


def transform(values):
    size = len(values)
    if size == 1:
        return values
    even, odd = transform(values[::2]), transform(values[1::2])
    low, high = [], []
    for k in range(size // 2):
        turned = odd[k]
        if 4 * k == size:
            turned = by_minus_i(turned)
        elif k:
            turned = times(
                turned,
                float(np.cos(2 * np.pi * k / size)),
                float(-np.sin(2 * np.pi * k / size)),
            )
        low.append(plus(even[k], turned))
        high.append(minus(even[k], turned))
    return low + high


def spectra(got_ref, high_ref, low_ref, twist_ref, out_ref, rows_high, rows_low, stage):
    for n2 in range(FAST):
        high, low = split(got_ref[n2])
        rows_high[pl.ds(n2 * PADDED, OWNED), :] = high
        rows_low[pl.ds(n2 * PADDED, OWNED), :] = low
    stage[...] = product(
        (rows_high[...], rows_low[...]), (high_ref[...], low_ref[...]), NN
    )
    tiles = STEPS // 2 // LANES
    for top in range(0, OWNED, 8):
        for left in range(0, SLOW, LANES):
            values = []
            for n2 in range(FAST):
                rows = pl.ds(n2 * PADDED + top, 8)
                value = (
                    stage[rows, pl.ds(left, LANES)],
                    stage[rows, pl.ds(SLOW + left, LANES)],
                )
                if n2:
                    lanes = pl.ds(left, LANES)
                    value = times(
                        value,
                        twist_ref[0, pl.ds(n2, 1), lanes],
                        twist_ref[1, pl.ds(n2, 1), lanes],
                    )
                values.append(value)
            valid = min(8, OWNED - top)
            for k2, value in enumerate(transform(values)[: FAST // 2]):
                tile = (k2 * SLOW + left) // LANES
                for part in range(2):
                    first = (top * tiles + tile) * 2 + part
                    to = pl.ds(first, valid, stride=2 * tiles)
                    out_ref[to, :] = value[part][:valid]


def call(kernel, shapes, *args, scratch=(), flops=0):
    whole = pl.BlockSpec(memory_space=pltpu.VMEM)
    return pl.pallas_call(
        kernel,
        out_shape=shapes,
        in_specs=[whole] * len(args),
        out_specs=jax.tree.map(lambda _: whole, shapes),
        scratch_shapes=scratch,
        compiler_params=pltpu.CompilerParams(vmem_limit_bytes=8 << 20),
        cost_estimate=pl.CostEstimate(
            flops=flops,
            transcendentals=0,
            bytes_accessed=sum(a.size * a.dtype.itemsize for a in args),
        ),
    )(*args)


def swap(x, axis):
    return lax.ppermute(x, axis, [(0, 1), (1, 0)])


def per_device(modal_history, stress_modes):
    modes, width = stress_modes.shape
    shape = jax.ShapeDtypeStruct
    vmem = pltpu.VMEM
    sent = call(
        scatter_steps,
        shape((SHARES, LANES // FAST, LANES), f32),
        modal_history.T,
        scratch=[vmem((LANES, LANES), f32)] * 2,
    )
    got = lax.all_to_all(sent, MODE, split_axis=0, concat_axis=0, tiled=True)
    pair = jnp.concatenate([stress_modes, swap(stress_modes, "yh")])
    quad = jnp.concatenate([pair, swap(pair, "c")])
    quads = [quad] + [
        lax.ppermute(quad, "x", [(i, (i + k) % 4) for i in range(4)]) for k in (1, 2, 3)
    ]
    high, low = call(
        order_modes,
        (shape((width, MODES), bf16), shape((width, MODES), bf16)),
        *quads,
        scratch=[vmem((MODES, width), f32)],
    )
    spread = call(join_shares, shape((BLOCKS, LANES // FAST, MODES), f32), got)
    steps = lax.all_to_all(spread, ELEM, split_axis=0, concat_axis=0, tiled=True)
    stress = call(contract, shape((SHARES, OWNED, SLOW), f32), high, low, steps)
    owned = lax.all_to_all(stress, MODE, split_axis=0, concat_axis=0, tiled=True)
    first_high, first_low, twist = tables()
    rows = FAST * PADDED
    out = call(
        spectra,
        shape((OWNED * STEPS // LANES, LANES), f32),
        owned,
        first_high,
        first_low,
        twist,
        scratch=[vmem((rows, SLOW), bf16)] * 2 + [vmem((rows, 2 * SLOW), f32)],
    )
    out = out.reshape(OWNED, STEPS // 2 // LANES, 2, LANES).transpose(0, 2, 1, 3)
    return out.reshape(OWNED, 2, STEPS // 2)


def solution(mesh):
    parts = Mesh(mesh.devices.reshape(SIZES), PARTS)
    return jax.shard_map(
        per_device,
        mesh=parts,
        in_specs=(P(ELEM, MODE), P(MODE, ELEM)),
        out_specs=P(PARTS, None, None),
        check_vma=False,
    )
```

time: 75 us -> 84 us (1.12)
  the two profiles are of different devices: /device:TPU:8 before, /device:TPU:1 now
where the time goes in v2:
time: 84 us; the launch traced here: 83.5 us
  blocking collectives  41.9 us (50%)
  starting transfers between devices  24.3 us (29%)
  waiting for transfers between devices  13.4 us (16%)
  Pallas kernels  2.89 us (3%)
    all_to_all x1, blocking collectives, per_device(): lax.all_to_all(stress, MODE, split_axis=0, concat_axis=0, tiled=True)  21.3 us
    all_to_all x1, blocking collectives, per_device(): got = lax.all_to_all(sent, MODE, split_axis=0, concat_axis=0, tiled=True)  20.6 us
    all_to_all x1, starting transfers between devices, per_device(): lax.all_to_all(spread, ELEM, split_axis=0, concat_axis=0, tiled=True)  11.1 us
    ppermute x2, waiting for transfers between devices, swap(): return lax.ppermute(x, axis, [(0, 1), (1, 0)])  8.43 us
    ppermute x3, starting transfers between devices, per_device(): lax.ppermute(quad, 'x', [(i, (i + k) % 4) for i in range(4)])  7.69 us
    ppermute x2, starting transfers between devices, swap(): return lax.ppermute(x, axis, [(0, 1), (1, 0)])  5.6 us
    ppermute x3, waiting for transfers between devices, per_device(): lax.ppermute(quad, 'x', [(i, (i + k) % 4) for i in range(4)])  4.99 us
    pallas_call x5, Pallas kernels, call(): pl.pallas_call(kernel, out_shape=shapes, in_specs=[whole] * len(args), ou...  2.89 us
  transfers between devices with their start and end apart: 6, of which 4 were waited for; matrix products, arithmetic and copies ran while one was open for 0% of the time, Pallas kernels for 0%

profile of v2, /device:TPU:1, one launch (start us, length us, event | category | flops | bytes accessed | tf_op | source)
XLA Modules:
  0.0 83.5 jit_solution(14236968344579729002)
XLA Ops:
  0.0 0.0 copy-start.3
  0.0 0.7 copy-done.3
  0.7 0.1 shard_map.56
  0.8 20.6 %all_to_all.15.got_ref = f32[16,8,128]{2,1,0:T(8,128)S(1)} all-to-all(f32[16,8,128]{2,1,0:T(8,128)S(1)} %shard_map.56), channel_id=1, replica_groups=mesh['z'=8,'yl'=4,'x'=4,'yh'=2,'c'=2] {'x','yh','c'}, dimensions={0} | all-to-all | bytes 131072 | tf_op jit(solution)/shard_map/all_to_all | solution.py:192
  21.4 0.9 %shard_map.57 = f32[32,8,512]{2,1,0:T(8,128)} custom-call(f32[16,8,128]{2,1,0:T(8,128)S(1)} %all_to_all.15.got_ref), custom_call_target="tpu_custom_call" | custom-call | bytes 65536 | tf_op jit(solution)/shard_map/pallas_call | solution.py:163
  22.3 0.0 copy-start.4
  22.3 11.1 %all-to-all-start.1 = ((f32[32,8,512]{2,1,0:T(8,128)}), f32[32,8,512]{2,1,0:T(8,128)S(1)}, u32[]{:S(2)}, u32[]{:S(2)}) async-start(f32[32,8,512]{2,1,0:T(8,128)} %shard_map.57), calls=%async_computation.1 | async-start | bytes 1048576 | tf_op jit(solution)/shard_map/all_to_all | solution.py:205
  33.4 0.0 copy-done.4
  33.4 2.4 %collective-permute-start = (f32[32,192]{1,0:T(8,128)S(1)}, f32[32,192]{1,0:T(8,128)S(1)}, u32[]{:S(2)}, u32[]{:S(2)}) collective-permute-start(f32[32,192]{1,0:T(8,128)S(1)} %copy-done.4), channel_id=1, source_target_pairs={{0,2},{2,0},{1,3},{3,1},{4,6},{6,4},{5,7},{7,5},{8,10},{10,8},{9,1... | collective-permute-start | bytes 73736 | tf_op jit(solution)/shard_map/ppermute | solution.py:179
  35.8 7.6 %collective-permute-done = f32[32,192]{1,0:T(8,128)S(1)} collective-permute-done((f32[32,192]{1,0:T(8,128)S(1)}, f32[32,192]{1,0:T(8,128)S(1)}, u32[]{:S(2)}, u32[]{:S(2)}) %collective-permute-start) | collective-permute-done | bytes 24608 | tf_op jit(solution)/shard_map/ppermute | solution.py:179
  43.3 3.2 %collective-permute-start.1 = (f32[64,192]{1,0:T(8,128)S(1)}, f32[64,192]{1,0:T(8,128)S(1)}, u32[]{:S(2)}, u32[]{:S(2)}) collective-permute-start(f32[64,192]{1,0:T(8,128)S(1)} %pad_maximum_fusion), channel_id=1, source_target_pairs={{0,1},{1,0},{2,3},{3,2},{4,5},{5,4},{6,7},{7,6},{8,9},{9,8},{10,11... | collective-permute-start | bytes 147464 | tf_op jit(solution)/shard_map/ppermute | solution.py:179
  46.6 0.9 %collective-permute-done.1 = f32[64,192]{1,0:T(8,128)S(1)} collective-permute-done((f32[64,192]{1,0:T(8,128)S(1)}, f32[64,192]{1,0:T(8,128)S(1)}, u32[]{:S(2)}, u32[]{:S(2)}) %collective-permute-start.1) | collective-permute-done | bytes 49184 | tf_op jit(solution)/shard_map/ppermute | solution.py:179
  47.5 2.7 %collective-permute-start.4 = (f32[128,192]{1,0:T(8,128)S(1)}, f32[128,192]{1,0:T(8,128)S(1)}, u32[]{:S(2)}, u32[]{:S(2)}) collective-permute-start(f32[128,192]{1,0:T(8,128)S(1)} %constant_dynamic-update-slice_fusion.own_ref), channel_id=1, source_target_pairs={{0,12},{4,0},{8,4},{12,8},{1,13},{5,1},{9,5},{13,9},{2,14},{6,2},{... | collective-permute-start | bytes 294920 | tf_op jit(solution)/shard_map/ppermute | solution.py:196
  50.2 3.1 %collective-permute-start.3 = (f32[128,192]{1,0:T(8,128)S(1)}, f32[128,192]{1,0:T(8,128)S(1)}, u32[]{:S(2)}, u32[]{:S(2)}) collective-permute-start(f32[128,192]{1,0:T(8,128)S(1)} %constant_dynamic-update-slice_fusion.own_ref), channel_id=1, source_target_pairs={{0,8},{4,12},{8,0},{12,4},{1,9},{5,13},{9,1},{13,5},{2,10},{6,14},... | collective-permute-start | bytes 294920 | tf_op jit(solution)/shard_map/ppermute | solution.py:196
  53.3 1.9 %collective-permute-start.2 = (f32[128,192]{1,0:T(8,128)S(1)}, f32[128,192]{1,0:T(8,128)S(1)}, u32[]{:S(2)}, u32[]{:S(2)}) collective-permute-start(f32[128,192]{1,0:T(8,128)S(1)} %constant_dynamic-update-slice_fusion.own_ref), channel_id=1, source_target_pairs={{0,4},{4,8},{8,12},{12,0},{1,5},{5,9},{9,13},{13,1},{2,6},{6,10},{... | collective-permute-start | bytes 294920 | tf_op jit(solution)/shard_map/ppermute | solution.py:196
  55.2 0.0 collective-permute-done.4.three_ref
  55.2 2.8 %collective-permute-done.3.two_ref = f32[128,192]{1,0:T(8,128)S(1)} collective-permute-done((f32[128,192]{1,0:T(8,128)S(1)}, f32[128,192]{1,0:T(8,128)S(1)}, u32[]{:S(2)}, u32[]{:S(2)}) %collective-permute-start.3) | collective-permute-done | bytes 98336 | tf_op jit(solution)/shard_map/ppermute | solution.py:196
  58.0 2.2 %collective-permute-done.2.one_ref = f32[128,192]{1,0:T(8,128)S(1)} collective-permute-done((f32[128,192]{1,0:T(8,128)S(1)}, f32[128,192]{1,0:T(8,128)S(1)}, u32[]{:S(2)}, u32[]{:S(2)}) %collective-permute-start.2) | collective-permute-done | bytes 98336 | tf_op jit(solution)/shard_map/ppermute | solution.py:196
  60.2 0.3 shard_map.55
  60.4 0.0 all-to-all-done.1.steps_ref
  60.5 0.0 copy-start.2
  60.5 0.4 shard_map.58
  60.9 0.0 copy-start
  60.9 0.0 copy-start.1
  60.9 21.3 %all_to_all.16.got_ref = f32[16,12,256]{2,1,0:T(8,128)S(1)} all-to-all(f32[16,12,256]{2,1,0:T(8,128)S(1)} %shard_map.58), channel_id=1, replica_groups=mesh['z'=8,'yl'=4,'x'=4,'yh'=2,'c'=2] {'x','yh','c'}, dimensions={0} | all-to-all | bytes 393216 | tf_op jit(solution)/shard_map/all_to_all | solution.py:207
  82.3 0.0 copy-done.2
  82.3 0.0 copy-done
  82.3 0.0 copy-done.1
  82.3 1.2 %shard_map.59 = f32[384,128]{1,0:T(8,128)} custom-call(f32[16,12,256]{2,1,0:T(8,128)S(1)} %all_to_all.16.got_ref, bf16[256,512]{1,0:T(8,128)(2,1)S(1)} %copy-done.1, bf16[256,512]{1,0:T(8,128)(2,1)S(1)} %copy-done, f32[2,16,256]{2,1,0:T(8,128)S(1)} %copy-done.2), custom_call_target="tpu_custom_call" | custom-call | bytes 753664 | tf_op jit(solution)/shard_map/pallas_call | solution.py:163
  (4 shorter events, 0.0 us)
Async XLA Ops:
  0.0 0.7 copy-start.3
  22.3 11.1 %copy-start.4 = (f32[32,192]{1,0:T(8,128)S(1)}, f32[32,192]{1,0:T(8,128)}, u32[]{:S(2)}) copy-start(f32[32,192]{1,0:T(8,128)} %param.6) | copy-start | bytes 73732
  22.3 38.1 %all-to-all-start.1 = ((f32[32,8,512]{2,1,0:T(8,128)}), f32[32,8,512]{2,1,0:T(8,128)S(1)}, u32[]{:S(2)}, u32[]{:S(2)}) async-start(f32[32,8,512]{2,1,0:T(8,128)} %shard_map.57), calls=%async_computation.1 | async-start | bytes 1048576 | tf_op jit(solution)/shard_map/all_to_all | solution.py:205
  33.4 9.9 %collective-permute-start = (f32[32,192]{1,0:T(8,128)S(1)}, f32[32,192]{1,0:T(8,128)S(1)}, u32[]{:S(2)}, u32[]{:S(2)}) collective-permute-start(f32[32,192]{1,0:T(8,128)S(1)} %copy-done.4), channel_id=1, source_target_pairs={{0,2},{2,0},{1,3},{3,1},{4,6},{6,4},{5,7},{7,5},{8,10},{10,8},{9,1... | collective-permute-start | bytes 73736 | tf_op jit(solution)/shard_map/ppermute | solution.py:179
  43.3 4.1 %collective-permute-start.1 = (f32[64,192]{1,0:T(8,128)S(1)}, f32[64,192]{1,0:T(8,128)S(1)}, u32[]{:S(2)}, u32[]{:S(2)}) collective-permute-start(f32[64,192]{1,0:T(8,128)S(1)} %pad_maximum_fusion), channel_id=1, source_target_pairs={{0,1},{1,0},{2,3},{3,2},{4,5},{5,4},{6,7},{7,6},{8,9},{9,8},{10,11... | collective-permute-start | bytes 147464 | tf_op jit(solution)/shard_map/ppermute | solution.py:179
  47.5 7.7 %collective-permute-start.4 = (f32[128,192]{1,0:T(8,128)S(1)}, f32[128,192]{1,0:T(8,128)S(1)}, u32[]{:S(2)}, u32[]{:S(2)}) collective-permute-start(f32[128,192]{1,0:T(8,128)S(1)} %constant_dynamic-update-slice_fusion.own_ref), channel_id=1, source_target_pairs={{0,12},{4,0},{8,4},{12,8},{1,13},{5,1},{9,5},{13,9},{2,14},{6,2},{... | collective-permute-start | bytes 294920 | tf_op jit(solution)/shard_map/ppermute | solution.py:196
  50.2 7.8 %collective-permute-start.3 = (f32[128,192]{1,0:T(8,128)S(1)}, f32[128,192]{1,0:T(8,128)S(1)}, u32[]{:S(2)}, u32[]{:S(2)}) collective-permute-start(f32[128,192]{1,0:T(8,128)S(1)} %constant_dynamic-update-slice_fusion.own_ref), channel_id=1, source_target_pairs={{0,8},{4,12},{8,0},{12,4},{1,9},{5,13},{9,1},{13,5},{2,10},{6,14},... | collective-permute-start | bytes 294920 | tf_op jit(solution)/shard_map/ppermute | solution.py:196
  53.3 6.9 %collective-permute-start.2 = (f32[128,192]{1,0:T(8,128)S(1)}, f32[128,192]{1,0:T(8,128)S(1)}, u32[]{:S(2)}, u32[]{:S(2)}) collective-permute-start(f32[128,192]{1,0:T(8,128)S(1)} %constant_dynamic-update-slice_fusion.own_ref), channel_id=1, source_target_pairs={{0,4},{4,8},{8,12},{12,0},{1,5},{5,9},{9,13},{13,1},{2,6},{6,10},{... | collective-permute-start | bytes 294920 | tf_op jit(solution)/shard_map/ppermute | solution.py:196
  60.5 21.8 %copy-start.2 = (f32[2,16,256]{2,1,0:T(8,128)S(1)}, f32[2,16,256]{2,1,0:T(8,128)}, u32[]{:S(2)}) copy-start(f32[2,16,256]{2,1,0:T(8,128)} %constant.8.clone.twist_ref) | copy-start | bytes 98308
  60.9 21.4 %copy-start = (bf16[256,512]{1,0:T(8,128)(2,1)S(1)}, bf16[256,512]{1,0:T(8,128)(2,1)}, u32[]{:S(2)}) copy-start(bf16[256,512]{1,0:T(8,128)(2,1)} %constant.7.clone.low_ref) | copy-start | bytes 786436
  60.9 21.4 %copy-start.1 = (bf16[256,512]{1,0:T(8,128)(2,1)S(1)}, bf16[256,512]{1,0:T(8,128)(2,1)}, u32[]{:S(2)}) copy-start(bf16[256,512]{1,0:T(8,128)(2,1)} %constant.6.clone.high_ref) | copy-start | bytes 786436

commit v3 on v2

--- a/solution.py
+++ b/solution.py
@@ -36,6 +36,8 @@
     k1 = np.arange(SLOW)
     angle = 2.0 * np.pi * ((k1[:, None] * k1[None, :]) % SLOW) / SLOW
     first = np.concatenate([np.cos(angle), -np.sin(angle)], axis=1) / np.sqrt(STEPS)
+    first = first.reshape(BLOCKS, 2, 4, 2 * SLOW).transpose(2, 0, 1, 3)
+    first = first.reshape(SLOW, 2 * SLOW)
     high = first.astype(np.float32).astype(jnp.bfloat16)
     low = (first - high.astype(np.float64)).astype(jnp.bfloat16)
     turn = 2.0 * np.pi * (np.arange(FAST)[:, None] * k1[None, :]) / STEPS
@@ -43,47 +45,60 @@
     return high, low, twist.astype(np.float32)
 
 
-def share():
-    return lax.axis_index(MODE)
-
-
 def scatter_steps(history_ref, out_ref, wide, tall):
     modes = history_ref.shape[0]
     wide[...] = jnp.zeros_like(wide)
-    at = pl.multiple_of(lax.rem(share(), LANES // modes) * modes, modes)
-    wide[pl.ds(at, modes), :] = history_ref[...]
+    wide[pl.ds(0, modes), :] = history_ref[...]
     tall[...] = wide[...].T
-    for n2 in range(FAST):
-        out_ref[n2] = tall[pl.ds(n2, LANES // FAST, stride=FAST), :]
-
-
-def join_shares(got_ref, out_ref):
-    for quad in range(4):
-        joined = (got_ref[4 * quad] + got_ref[4 * quad + 1]) + (
-            got_ref[4 * quad + 2] + got_ref[4 * quad + 3]
-        )
-        lanes = pl.ds(quad * LANES, LANES)
-        out_ref[:, :, lanes] = jnp.broadcast_to(joined, (BLOCKS,) + joined.shape)
-
-
-def order_modes(own_ref, one_ref, two_ref, three_ref, high_ref, low_ref, whole):
+    turn = lax.rem(lax.axis_index(MODE), 4)
+    for half in range(2):
+        joined = None
+        for quarter in range(4):
+            rows = tall[pl.ds((4 * half + quarter) * FAST, FAST), :]
+            rows = pltpu.roll(rows, lax.rem(quarter + turn, 4) * modes, 1)
+            joined = rows if joined is None else joined + rows
+        wide[pl.ds(half * FAST, FAST), :] = joined
+    odd = lax.broadcasted_iota(jnp.int32, (2 * BLOCKS, LANES), 0) % 2 == 1
+    for owner in range(SHARES):
+        first = jnp.broadcast_to(wide[pl.ds(owner, 1), :], odd.shape)
+        second = jnp.broadcast_to(wide[pl.ds(FAST + owner, 1), :], odd.shape)
+        out_ref[pl.ds(owner * 2 * BLOCKS, 2 * BLOCKS), :] = jnp.where(odd, second, first)
+
+
+def order_modes(own_ref, y_ref, c_ref, both_ref, high_ref, low_ref, whole):
     x, y, c = lax.axis_index("x"), lax.axis_index("yh"), lax.axis_index("c")
     rows = own_ref.shape[0] // 4
-    for shift, ref in enumerate((own_ref, one_ref, two_ref, three_ref)):
-        at_x = lax.rem(x + 4 - shift, 4)
-        for part in range(4):
-            at_y = lax.rem(y + part % 2, 2)
-            at_c = lax.rem(c + part // 2, 2)
+    for other, ref in enumerate((own_ref, y_ref, c_ref, both_ref)):
+        at_y = lax.rem(y + other % 2, 2)
+        at_c = lax.rem(c + other // 2, 2)
+        for shift in range(4):
+            at_x = lax.rem(x + 4 - shift, 4)
             at = pl.multiple_of((at_x * 4 + at_y * 2 + at_c) * rows, rows)
-            whole[pl.ds(at, rows), :] = ref[pl.ds(part * rows, rows), :]
+            whole[pl.ds(at, rows), :] = ref[pl.ds(shift * rows, rows), :]
     high_ref[...], low_ref[...] = split(whole[...].T)
 
 
-def contract(high_ref, low_ref, steps_ref, out_ref):
-    steps = steps_ref[...].reshape(SLOW, MODES)
-    stress = product((high_ref[...], low_ref[...]), split(steps), NT)
+def contract(high_ref, low_ref, got_ref, out_ref, steps_high, steps_low):
+    rows = 2 * BLOCKS
+    block = lax.broadcasted_iota(jnp.int32, (rows, LANES), 1) // (LANES // 4)
+    for quad in range(SHARES // 4):
+        shares = [got_ref[pl.ds((4 * quad + k) * rows, rows), :] for k in range(4)]
+        for quarter in range(4):
+            value = shares[-quarter % 4]
+            for k in range(1, 4):
+                value = jnp.where(block == k, shares[(k - quarter) % 4], value)
+            if quarter:
+                value = pltpu.roll(value, LANES - quarter * LANES // 4, 1)
+            at = (pl.ds(quarter * rows, rows), pl.ds(quad * LANES, LANES))
+            steps_high[at], steps_low[at] = split(value)
+    stress = product(
+        (high_ref[...], low_ref[...]), (steps_high[...], steps_low[...]), NT
+    )
     for owner in range(SHARES):
-        out_ref[owner] = stress[owner * OWNED : (owner + 1) * OWNED, :]
+        for tile in range(SLOW // LANES):
+            out_ref[owner, pl.ds(tile * OWNED, OWNED), :] = stress[
+                owner * OWNED : (owner + 1) * OWNED, tile * LANES : (tile + 1) * LANES
+            ]
 
 
 def plus(a, b):
@@ -125,9 +140,10 @@
 
 def spectra(got_ref, high_ref, low_ref, twist_ref, out_ref, rows_high, rows_low, stage):
     for n2 in range(FAST):
-        high, low = split(got_ref[n2])
-        rows_high[pl.ds(n2 * PADDED, OWNED), :] = high
-        rows_low[pl.ds(n2 * PADDED, OWNED), :] = low
+        for tile in range(SLOW // LANES):
+            at = (pl.ds(n2 * PADDED, OWNED), pl.ds(tile * LANES, LANES))
+            value = got_ref[n2, pl.ds(tile * OWNED, OWNED), :]
+            rows_high[at], rows_low[at] = split(value)
     stage[...] = product(
         (rows_high[...], rows_low[...]), (high_ref[...], low_ref[...]), NN
     )
@@ -185,25 +201,40 @@
     vmem = pltpu.VMEM
     sent = call(
         scatter_steps,
-        shape((SHARES, LANES // FAST, LANES), f32),
+        shape((SHARES * BLOCKS * 2, LANES), f32),
         modal_history.T,
         scratch=[vmem((LANES, LANES), f32)] * 2,
     )
-    got = lax.all_to_all(sent, MODE, split_axis=0, concat_axis=0, tiled=True)
-    pair = jnp.concatenate([stress_modes, swap(stress_modes, "yh")])
-    quad = jnp.concatenate([pair, swap(pair, "c")])
-    quads = [quad] + [
-        lax.ppermute(quad, "x", [(i, (i + k) % 4) for i in range(4)]) for k in (1, 2, 3)
+    got = lax.all_to_all(
+        sent.reshape(SHARES * BLOCKS, 2, LANES),
+        MODE + ELEM,
+        split_axis=0,
+        concat_axis=0,
+        tiled=True,
+    )
+    near = [stress_modes] + [
+        lax.ppermute(stress_modes, "x", [(i, (i + k) % 4) for i in range(4)])
+        for k in (1, 2, 3)
     ]
+    near = jnp.concatenate(near)
+    across = [(i, i ^ 3) for i in range(4)]
     high, low = call(
         order_modes,
         (shape((width, MODES), bf16), shape((width, MODES), bf16)),
-        *quads,
+        near,
+        swap(near, "yh"),
+        swap(near, "c"),
+        lax.ppermute(near, ("yh", "c"), across),
         scratch=[vmem((MODES, width), f32)],
     )
-    spread = call(join_shares, shape((BLOCKS, LANES // FAST, MODES), f32), got)
-    steps = lax.all_to_all(spread, ELEM, split_axis=0, concat_axis=0, tiled=True)
-    stress = call(contract, shape((SHARES, OWNED, SLOW), f32), high, low, steps)
+    stress = call(
+        contract,
+        shape((SHARES, SLOW // LANES * OWNED, LANES), f32),
+        high,
+        low,
+        got.reshape(SHARES * BLOCKS * 2, LANES),
+        scratch=[vmem((SLOW, MODES), bf16)] * 2,
+    )
     owned = lax.all_to_all(stress, MODE, split_axis=0, concat_axis=0, tiled=True)
     first_high, first_low, twist = tables()
     rows = FAST * PADDED

time: 84 us -> 80.8 us (0.962)
  the two profiles are of different devices: /device:TPU:1 before, /device:TPU:17 now
where the time goes in v3:
time: 80.8 us; the launch traced here: 80.3 us
  starting transfers between devices  45.2 us (56%)
  blocking collectives  23.1 us (29%)
  waiting for transfers between devices  7.97 us (10%)
  Pallas kernels  3.08 us (4%)
    all_to_all x1, blocking collectives, per_device(): lax.all_to_all(stress, MODE, split_axis=0, concat_axis=0, tiled=True)  23.1 us
    all_to_all x1, starting transfers between devices, per_device(): lax.all_to_all(sent.reshape(SHARES * BLOCKS, 2, LANES), MODE + ELEM, spli...  21.3 us
    ppermute x3, starting transfers between devices, per_device(): lax.ppermute(stress_modes, 'x', [(i, (i + k) % 4) for i in range(4)])  11.1 us
    ppermute x1, starting transfers between devices, per_device(): lax.ppermute(near, ('yh', 'c'), across)  7.12 us
    ppermute x2, waiting for transfers between devices, swap(): return lax.ppermute(x, axis, [(0, 1), (1, 0)])  6.88 us
    ppermute x2, starting transfers between devices, swap(): return lax.ppermute(x, axis, [(0, 1), (1, 0)])  5.64 us
    pallas_call x4, Pallas kernels, call(): pl.pallas_call(kernel, out_shape=shapes, in_specs=[whole] * len(args), ou...  3.08 us
  transfers between devices with their start and end apart: 7, of which 3 were waited for; matrix products, arithmetic and copies ran while one was open for 0% of the time, Pallas kernels for 0%

profile of v3, /device:TPU:17, one launch (start us, length us, event | category | flops | bytes accessed | tf_op | source)
XLA Modules:
  0.0 80.3 jit_solution(7548472685608383441)
XLA Ops:
  0.0 0.0 copy-start.3
  0.0 0.7 copy-done.3
  0.7 1.0 %shard_map.56 = f32[1024,128]{1,0:T(8,128)} custom-call(f32[32,128]{1,0:T(8,128)S(1)} %bitcast.9), custom_call_target="tpu_custom_call" | custom-call | bytes 16384 | tf_op jit(solution)/shard_map/pallas_call | solution.py:179
  1.7 0.0 copy-start.4
  1.7 21.3 %all-to-all-start = ((f32[512,2,128]{2,1,0:T(2,128)}), f32[512,2,128]{2,1,0:T(2,128)S(1)}, u32[]{:S(2)}, u32[]{:S(2)}) async-start(f32[512,2,128]{2,1,0:T(2,128)} %bitcast.1), calls=%async_computation | async-start | bytes 1048576 | tf_op jit(solution)/shard_map/all_to_all | solution.py:208
  23.0 0.0 copy-done.4
  23.1 4.6 %collective-permute-start.1 = (f32[32,192]{1,0:T(8,128)S(1)}, f32[32,192]{1,0:T(8,128)S(1)}, u32[]{:S(2)}, u32[]{:S(2)}) collective-permute-start(f32[32,192]{1,0:T(8,128)S(1)} %copy-done.4), channel_id=1, source_target_pairs={{0,8},{4,12},{8,0},{12,4},{1,9},{5,13},{9,1},{13,5},{2,10},{6,14},... | collective-permute-start | bytes 73736 | tf_op jit(solution)/shard_map/ppermute | solution.py:216
  27.7 2.2 %collective-permute-start = (f32[32,192]{1,0:T(8,128)S(1)}, f32[32,192]{1,0:T(8,128)S(1)}, u32[]{:S(2)}, u32[]{:S(2)}) collective-permute-start(f32[32,192]{1,0:T(8,128)S(1)} %copy-done.4), channel_id=1, source_target_pairs={{0,4},{4,8},{8,12},{12,0},{1,5},{5,9},{9,13},{13,1},{2,6},{6,10},{... | collective-permute-start | bytes 73736 | tf_op jit(solution)/shard_map/ppermute | solution.py:216
  29.9 4.3 %collective-permute-start.2 = (f32[32,192]{1,0:T(8,128)S(1)}, f32[32,192]{1,0:T(8,128)S(1)}, u32[]{:S(2)}, u32[]{:S(2)}) collective-permute-start(f32[32,192]{1,0:T(8,128)S(1)} %copy-done.4), channel_id=1, source_target_pairs={{0,12},{4,0},{8,4},{12,8},{1,13},{5,1},{9,5},{13,9},{2,14},{6,2},{... | collective-permute-start | bytes 73736 | tf_op jit(solution)/shard_map/ppermute | solution.py:216
  34.2 0.0 collective-permute-done
  34.2 0.0 collective-permute-done.1
  34.2 0.9 %collective-permute-done.2 = f32[32,192]{1,0:T(8,128)S(1)} collective-permute-done((f32[32,192]{1,0:T(8,128)S(1)}, f32[32,192]{1,0:T(8,128)S(1)}, u32[]{:S(2)}, u32[]{:S(2)}) %collective-permute-start.2) | collective-permute-done | bytes 24608 | tf_op jit(solution)/shard_map/ppermute | solution.py:216
  35.2 7.1 %collective-permute-start.5 = (f32[128,192]{1,0:T(8,128)S(1)}, f32[128,192]{1,0:T(8,128)S(1)}, u32[]{:S(2)}, u32[]{:S(2)}) collective-permute-start(f32[128,192]{1,0:T(8,128)S(1)} %constant_dynamic-update-slice_fusion.own_ref), channel_id=1, source_target_pairs={{0,3},{1,2},{2,1},{3,0},{4,7},{5,6},{6,5},{7,4},{8,11},{9,10},{10,... | collective-permute-start | bytes 294920 | tf_op jit(solution)/shard_map/ppermute | solution.py:227
  42.3 1.9 %collective-permute-start.4 = (f32[128,192]{1,0:T(8,128)S(1)}, f32[128,192]{1,0:T(8,128)S(1)}, u32[]{:S(2)}, u32[]{:S(2)}) collective-permute-start(f32[128,192]{1,0:T(8,128)S(1)} %constant_dynamic-update-slice_fusion.own_ref), channel_id=1, source_target_pairs={{0,1},{1,0},{2,3},{3,2},{4,5},{5,4},{6,7},{7,6},{8,9},{9,8},{10,11... | collective-permute-start | bytes 294920 | tf_op jit(solution)/shard_map/ppermute | solution.py:195
  44.2 3.7 %collective-permute-start.3 = (f32[128,192]{1,0:T(8,128)S(1)}, f32[128,192]{1,0:T(8,128)S(1)}, u32[]{:S(2)}, u32[]{:S(2)}) collective-permute-start(f32[128,192]{1,0:T(8,128)S(1)} %constant_dynamic-update-slice_fusion.own_ref), channel_id=1, source_target_pairs={{0,2},{2,0},{1,3},{3,1},{4,6},{6,4},{5,7},{7,5},{8,10},{10,8},{9,1... | collective-permute-start | bytes 294920 | tf_op jit(solution)/shard_map/ppermute | solution.py:195
  48.0 0.1 collective-permute-done.5.both_ref
  48.1 0.0 collective-permute-done.4.c_ref
  48.1 6.9 %collective-permute-done.3.y_ref = f32[128,192]{1,0:T(8,128)S(1)} collective-permute-done((f32[128,192]{1,0:T(8,128)S(1)}, f32[128,192]{1,0:T(8,128)S(1)}, u32[]{:S(2)}, u32[]{:S(2)}) %collective-permute-start.3) | collective-permute-done | bytes 98336 | tf_op jit(solution)/shard_map/ppermute | solution.py:195
  55.0 0.3 shard_map.55
  55.3 0.0 all-to-all-done
  55.3 0.0 copy-start.1
  55.3 0.6 shard_map.57
  55.9 0.0 copy-start
  55.9 0.0 copy-start.2
  55.9 23.1 %all_to_all.10.got_ref = f32[16,24,128]{2,1,0:T(8,128)S(1)} all-to-all(f32[16,24,128]{2,1,0:T(8,128)S(1)} %shard_map.57), channel_id=1, replica_groups=mesh['z'=8,'yl'=4,'x'=4,'yh'=2,'c'=2] {'x','yh','c'}, dimensions={0} | all-to-all | bytes 393216 | tf_op jit(solution)/shard_map/all_to_all | solution.py:238
  79.0 0.0 copy-done.1
  79.0 0.0 copy-done
  79.0 0.0 copy-done.2
  79.0 1.2 %shard_map.58 = f32[384,128]{1,0:T(8,128)} custom-call(f32[16,24,128]{2,1,0:T(8,128)S(1)} %all_to_all.10.got_ref, bf16[256,512]{1,0:T(8,128)(2,1)S(1)} %copy-done.1, bf16[256,512]{1,0:T(8,128)(2,1)S(1)} %copy-done, f32[2,16,256]{2,1,0:T(8,128)S(1)} %copy-done.2), custom_call_target="tpu_custom_call" | custom-call | bytes 753664 | tf_op jit(solution)/shard_map/pallas_call | solution.py:179
  (4 shorter events, 0.0 us)
Async XLA Ops:
  0.0 0.7 copy-start.3
  1.7 21.3 %copy-start.4 = (f32[32,192]{1,0:T(8,128)S(1)}, f32[32,192]{1,0:T(8,128)}, u32[]{:S(2)}) copy-start(f32[32,192]{1,0:T(8,128)} %param.6) | copy-start | bytes 73732
  1.7 53.5 %all-to-all-start = ((f32[512,2,128]{2,1,0:T(2,128)}), f32[512,2,128]{2,1,0:T(2,128)S(1)}, u32[]{:S(2)}, u32[]{:S(2)}) async-start(f32[512,2,128]{2,1,0:T(2,128)} %bitcast.1), calls=%async_computation | async-start | bytes 1048576 | tf_op jit(solution)/shard_map/all_to_all | solution.py:208
  23.1 11.2 %collective-permute-start.1 = (f32[32,192]{1,0:T(8,128)S(1)}, f32[32,192]{1,0:T(8,128)S(1)}, u32[]{:S(2)}, u32[]{:S(2)}) collective-permute-start(f32[32,192]{1,0:T(8,128)S(1)} %copy-done.4), channel_id=1, source_target_pairs={{0,8},{4,12},{8,0},{12,4},{1,9},{5,13},{9,1},{13,5},{2,10},{6,14},... | collective-permute-start | bytes 73736 | tf_op jit(solution)/shard_map/ppermute | solution.py:216
  27.7 6.5 %collective-permute-start = (f32[32,192]{1,0:T(8,128)S(1)}, f32[32,192]{1,0:T(8,128)S(1)}, u32[]{:S(2)}, u32[]{:S(2)}) collective-permute-start(f32[32,192]{1,0:T(8,128)S(1)} %copy-done.4), channel_id=1, source_target_pairs={{0,4},{4,8},{8,12},{12,0},{1,5},{5,9},{9,13},{13,1},{2,6},{6,10},{... | collective-permute-start | bytes 73736 | tf_op jit(solution)/shard_map/ppermute | solution.py:216
  29.9 5.3 %collective-permute-start.2 = (f32[32,192]{1,0:T(8,128)S(1)}, f32[32,192]{1,0:T(8,128)S(1)}, u32[]{:S(2)}, u32[]{:S(2)}) collective-permute-start(f32[32,192]{1,0:T(8,128)S(1)} %copy-done.4), channel_id=1, source_target_pairs={{0,12},{4,0},{8,4},{12,8},{1,13},{5,1},{9,5},{13,9},{2,14},{6,2},{... | collective-permute-start | bytes 73736 | tf_op jit(solution)/shard_map/ppermute | solution.py:216
  35.2 12.9 %collective-permute-start.5 = (f32[128,192]{1,0:T(8,128)S(1)}, f32[128,192]{1,0:T(8,128)S(1)}, u32[]{:S(2)}, u32[]{:S(2)}) collective-permute-start(f32[128,192]{1,0:T(8,128)S(1)} %constant_dynamic-update-slice_fusion.own_ref), channel_id=1, source_target_pairs={{0,3},{1,2},{2,1},{3,0},{4,7},{5,6},{6,5},{7,4},{8,11},{9,10},{10,... | collective-permute-start | bytes 294920 | tf_op jit(solution)/shard_map/ppermute | solution.py:227
  42.3 5.8 %collective-permute-start.4 = (f32[128,192]{1,0:T(8,128)S(1)}, f32[128,192]{1,0:T(8,128)S(1)}, u32[]{:S(2)}, u32[]{:S(2)}) collective-permute-start(f32[128,192]{1,0:T(8,128)S(1)} %constant_dynamic-update-slice_fusion.own_ref), channel_id=1, source_target_pairs={{0,1},{1,0},{2,3},{3,2},{4,5},{5,4},{6,7},{7,6},{8,9},{9,8},{10,11... | collective-permute-start | bytes 294920 | tf_op jit(solution)/shard_map/ppermute | solution.py:195
  44.2 10.7 %collective-permute-start.3 = (f32[128,192]{1,0:T(8,128)S(1)}, f32[128,192]{1,0:T(8,128)S(1)}, u32[]{:S(2)}, u32[]{:S(2)}) collective-permute-start(f32[128,192]{1,0:T(8,128)S(1)} %constant_dynamic-update-slice_fusion.own_ref), channel_id=1, source_target_pairs={{0,2},{2,0},{1,3},{3,1},{4,6},{6,4},{5,7},{7,5},{8,10},{10,8},{9,1... | collective-permute-start | bytes 294920 | tf_op jit(solution)/shard_map/ppermute | solution.py:195
  55.3 23.8 %copy-start.1 = (bf16[256,512]{1,0:T(8,128)(2,1)S(1)}, bf16[256,512]{1,0:T(8,128)(2,1)}, u32[]{:S(2)}) copy-start(bf16[256,512]{1,0:T(8,128)(2,1)} %constant.6.clone.high_ref) | copy-start | bytes 786436
  55.9 23.2 %copy-start = (bf16[256,512]{1,0:T(8,128)(2,1)S(1)}, bf16[256,512]{1,0:T(8,128)(2,1)}, u32[]{:S(2)}) copy-start(bf16[256,512]{1,0:T(8,128)(2,1)} %constant.7.clone.low_ref) | copy-start | bytes 786436
  55.9 23.1 %copy-start.2 = (f32[2,16,256]{2,1,0:T(8,128)S(1)}, f32[2,16,256]{2,1,0:T(8,128)}, u32[]{:S(2)}) copy-start(f32[2,16,256]{2,1,0:T(8,128)} %constant.8.clone.twist_ref) | copy-start | bytes 98308

commit v4 on v2

--- a/solution.py
+++ b/solution.py
@@ -11,8 +11,9 @@
 SIZES = (8, 4, 4, 2, 2)
 ELEM = ("z", "yl")
 MODE = ("x", "yh", "c")
-BLOCKS, SHARES = 32, 16
-STEPS, MODES = 4096, 512
+PAIR = ("x", "c")
+BLOCKS, SHARES, PAIRS = 32, 16, 8
+STEPS, MODES = 4096, 256
 SLOW, FAST = 256, 16
 OWNED, PADDED = 12, 16
 LANES = 128
@@ -43,47 +44,71 @@
     return high, low, twist.astype(np.float32)
 
 
-def share():
-    return lax.axis_index(MODE)
-
-
-def scatter_steps(history_ref, out_ref, wide, tall):
-    modes = history_ref.shape[0]
+def scatter(history_hbm, modes_hbm, out_ref, wide, tall, modes_ref, arrived):
+    modes, width = modes_ref.shape
     wide[...] = jnp.zeros_like(wide)
-    at = pl.multiple_of(lax.rem(share(), LANES // modes) * modes, modes)
-    wide[pl.ds(at, modes), :] = history_ref[...]
+    at = pl.multiple_of(lax.rem(lax.axis_index(PAIR), LANES // modes) * modes, modes)
+    copies = (
+        pltpu.make_async_copy(history_hbm, wide.at[pl.ds(at, modes), :], arrived.at[0]),
+        pltpu.make_async_copy(modes_hbm, modes_ref, arrived.at[1]),
+    )
+    for copy in copies:
+        copy.start()
+    for copy in copies:
+        copy.wait()
     tall[...] = wide[...].T
-    for n2 in range(FAST):
-        out_ref[n2] = tall[pl.ds(n2, LANES // FAST, stride=FAST), :]
-
-
-def join_shares(got_ref, out_ref):
-    for quad in range(4):
-        joined = (got_ref[4 * quad] + got_ref[4 * quad + 1]) + (
-            got_ref[4 * quad + 2] + got_ref[4 * quad + 3]
-        )
+    half = modes // 2
+    for pair in range(PAIRS):
+        for high in range(2):
+            rows = tall[pl.ds(8 * high + pair, LANES // FAST, stride=FAST), :]
+            out_ref[pair, pl.ds(high * 8, 8), :] = rows
+        first = (pair % 2) * half
+        out_ref[pair, pl.ds(16, half), :] = modes_ref[pl.ds(first, half), :LANES]
+        rest = width - LANES
+        for side in range(2):
+            out_ref[pair, pl.ds(16 + half, 8), pl.ds(side * rest, rest)] = modes_ref[
+                pl.ds(first + side * 8, 8), LANES:
+            ]
+
+
+def spread(got_ref, out_ref):
+    for quad in range(PAIRS // 4):
+        joined = None
+        for sender in range(4 * quad, 4 * quad + 4):
+            rows = got_ref[sender, pl.ds(0, 16), :]
+            joined = rows if joined is None else joined + rows
         lanes = pl.ds(quad * LANES, LANES)
         out_ref[:, :, lanes] = jnp.broadcast_to(joined, (BLOCKS,) + joined.shape)
 
 
-def order_modes(own_ref, one_ref, two_ref, three_ref, high_ref, low_ref, whole):
-    x, y, c = lax.axis_index("x"), lax.axis_index("yh"), lax.axis_index("c")
-    rows = own_ref.shape[0] // 4
-    for shift, ref in enumerate((own_ref, one_ref, two_ref, three_ref)):
-        at_x = lax.rem(x + 4 - shift, 4)
-        for part in range(4):
-            at_y = lax.rem(y + part % 2, 2)
-            at_c = lax.rem(c + part // 2, 2)
-            at = pl.multiple_of((at_x * 4 + at_y * 2 + at_c) * rows, rows)
-            whole[pl.ds(at, rows), :] = ref[pl.ds(part * rows, rows), :]
+def order_modes(own_ref, other_ref, high_ref, low_ref, whole):
+    c = lax.axis_index("c")
+    half = MODES // PAIRS // 2
+    rest = whole.shape[1] - LANES
+    for ref, which in ((own_ref, c), (other_ref, 1 - c)):
+        for sender in range(PAIRS):
+            at = pl.multiple_of(sender * 2 * half + which * half, half)
+            whole[pl.ds(at, half), pl.ds(0, LANES)] = ref[sender, pl.ds(0, half), :]
+            for side in range(2):
+                rows = pl.ds(pl.multiple_of(at + side * 8, 8), 8)
+                whole[rows, pl.ds(LANES, rest)] = ref[
+                    sender, pl.ds(half, 8), pl.ds(side * rest, rest)
+                ]
     high_ref[...], low_ref[...] = split(whole[...].T)
 
 
 def contract(high_ref, low_ref, steps_ref, out_ref):
-    steps = steps_ref[...].reshape(SLOW, MODES)
-    stress = product((high_ref[...], low_ref[...]), split(steps), NT)
-    for owner in range(SHARES):
-        out_ref[owner] = stress[owner * OWNED : (owner + 1) * OWNED, :]
+    modes = (high_ref[...], low_ref[...])
+    tiles = SLOW // LANES
+    for high in range(2):
+        steps = steps_ref[:, pl.ds(8 * high, 8), :].reshape(SLOW, MODES)
+        stress = product(modes, split(steps), NT)
+        for owner in range(SHARES):
+            for tile in range(tiles):
+                out_ref[owner, pl.ds((high * tiles + tile) * OWNED, OWNED), :] = stress[
+                    owner * OWNED : (owner + 1) * OWNED,
+                    tile * LANES : (tile + 1) * LANES,
+                ]
 
 
 def plus(a, b):
@@ -125,9 +150,12 @@
 
 def spectra(got_ref, high_ref, low_ref, twist_ref, out_ref, rows_high, rows_low, stage):
     for n2 in range(FAST):
-        high, low = split(got_ref[n2])
-        rows_high[pl.ds(n2 * PADDED, OWNED), :] = high
-        rows_low[pl.ds(n2 * PADDED, OWNED), :] = low
+        for tile in range(SLOW // LANES):
+            at = (pl.ds(n2 * PADDED, OWNED), pl.ds(tile * LANES, LANES))
+            sender = (n2 % 8) // 2 * 4 + n2 % 2
+            part = pl.ds((n2 // 8 * 2 + tile) * OWNED, OWNED)
+            value = got_ref[sender, part, :] + got_ref[sender + 2, part, :]
+            rows_high[at], rows_low[at] = split(value)
     stage[...] = product(
         (rows_high[...], rows_low[...]), (high_ref[...], low_ref[...]), NN
     )
@@ -158,25 +186,21 @@
                     out_ref[to, :] = value[part][:valid]
 
 
-def call(kernel, shapes, *args, scratch=(), flops=0):
+def call(kernel, shapes, *args, scratch=(), space=pltpu.VMEM, limit=8 << 20):
     whole = pl.BlockSpec(memory_space=pltpu.VMEM)
     return pl.pallas_call(
         kernel,
         out_shape=shapes,
-        in_specs=[whole] * len(args),
+        in_specs=[pl.BlockSpec(memory_space=space)] * len(args),
         out_specs=jax.tree.map(lambda _: whole, shapes),
         scratch_shapes=scratch,
-        compiler_params=pltpu.CompilerParams(vmem_limit_bytes=8 << 20),
+        compiler_params=pltpu.CompilerParams(vmem_limit_bytes=limit),
         cost_estimate=pl.CostEstimate(
-            flops=flops,
+            flops=0,
             transcendentals=0,
             bytes_accessed=sum(a.size * a.dtype.itemsize for a in args),
         ),
     )(*args)
-
-
-def swap(x, axis):
-    return lax.ppermute(x, axis, [(0, 1), (1, 0)])
 
 
 def per_device(modal_history, stress_modes):
@@ -184,26 +208,33 @@
     shape = jax.ShapeDtypeStruct
     vmem = pltpu.VMEM
     sent = call(
-        scatter_steps,
-        shape((SHARES, LANES // FAST, LANES), f32),
+        scatter,
+        shape((PAIRS, 16 + 24, LANES), f32),
         modal_history.T,
-        scratch=[vmem((LANES, LANES), f32)] * 2,
-    )
-    got = lax.all_to_all(sent, MODE, split_axis=0, concat_axis=0, tiled=True)
-    pair = jnp.concatenate([stress_modes, swap(stress_modes, "yh")])
-    quad = jnp.concatenate([pair, swap(pair, "c")])
-    quads = [quad] + [
-        lax.ppermute(quad, "x", [(i, (i + k) % 4) for i in range(4)]) for k in (1, 2, 3)
-    ]
+        stress_modes,
+        scratch=[vmem((LANES, LANES), f32)] * 2
+        + [vmem((modes, width), f32), pltpu.SemaphoreType.DMA((2,))],
+        space=pltpu.HBM,
+        limit=60 << 20,
+    )
+    got = lax.all_to_all(sent, PAIR, split_axis=0, concat_axis=0, tiled=True)
+    history = call(spread, shape((BLOCKS, 16, MODES), f32), got)
+    steps = lax.all_to_all(history, ELEM, split_axis=0, concat_axis=0, tiled=True)
+    own = got[:, 16:]
     high, low = call(
         order_modes,
         (shape((width, MODES), bf16), shape((width, MODES), bf16)),
-        *quads,
+        own,
+        lax.ppermute(own, "c", [(0, 1), (1, 0)]),
         scratch=[vmem((MODES, width), f32)],
     )
-    spread = call(join_shares, shape((BLOCKS, LANES // FAST, MODES), f32), got)
-    steps = lax.all_to_all(spread, ELEM, split_axis=0, concat_axis=0, tiled=True)
-    stress = call(contract, shape((SHARES, OWNED, SLOW), f32), high, low, steps)
+    stress = call(
+        contract,
+        shape((SHARES, 2 * SLOW // LANES * OWNED, LANES), f32),
+        high,
+        low,
+        steps,
+    )
     owned = lax.all_to_all(stress, MODE, split_axis=0, concat_axis=0, tiled=True)
     first_high, first_low, twist = tables()
     rows = FAST * PADDED

time: 84 us -> 68.6 us (0.82)
  the two profiles are of different devices: /device:TPU:1 before, /device:TPU:8 now
where the time goes in v4:
time: 68.6 us; the launch traced here: 68.2 us
  blocking collectives  33.4 us (49%)
  starting transfers between devices  15.9 us (23%)
  waiting for transfers between devices  14.5 us (21%)
  Pallas kernels  4.31 us (6%)
    all_to_all x1, blocking collectives, per_device(): lax.all_to_all(stress, MODE, split_axis=0, concat_axis=0, tiled=True)  22.6 us
    all_to_all x1, starting transfers between devices, per_device(): lax.all_to_all(history, ELEM, split_axis=0, concat_axis=0, tiled=True)  14 us
    all_to_all x1, waiting for transfers between devices, per_device(): lax.all_to_all(history, ELEM, split_axis=0, concat_axis=0, tiled=True)  13.2 us
    all_to_all x1, blocking collectives, per_device(): got = lax.all_to_all(sent, PAIR, split_axis=0, concat_axis=0, tiled=True)  10.8 us
    pallas_call x5, Pallas kernels, call(): pl.pallas_call(kernel, out_shape=shapes, in_specs=[pl.BlockSpec(memory_sp...  4.31 us
    ppermute x1, starting transfers between devices, per_device(): lax.ppermute(own, 'c', [(0, 1), (1, 0)])  1.92 us
  transfers between devices with their start and end apart: 2, of which 2 were waited for; matrix products, arithmetic and copies ran while one was open for 0% of the time, Pallas kernels for 0%

profile of v4, /device:TPU:8, one launch (start us, length us, event | category | flops | bytes accessed | tf_op | source)
XLA Modules:
  0.0 68.2 jit_solution(15173065839535546421)
XLA Ops:
  0.0 1.6 %shard_map.55 = f32[8,40,128]{2,1,0:T(8,128)} custom-call(f32[32,128]{1,0:T(8,128)} %bitcast.6, f32[32,192]{1,0:T(8,128)} %modes_hbm.1), custom_call_target="tpu_custom_call" | custom-call | bytes 40960 | tf_op jit(solution)/shard_map/pallas_call | solution.py:191
  1.6 10.8 %all_to_all.15.got_ref = f32[8,40,128]{2,1,0:T(8,128)S(1)} all-to-all(f32[8,40,128]{2,1,0:T(8,128)} %shard_map.55), channel_id=1, replica_groups=mesh['z'=8,'yl'=4,'x'=4,'yh'=2,'c'=2] {'x','c'}, dimensions={0} | all-to-all | bytes 327680 | tf_op jit(solution)/shard_map/all_to_all | solution.py:220
  12.4 0.9 %shard_map.57 = f32[32,16,256]{2,1,0:T(8,128)} custom-call(f32[8,40,128]{2,1,0:T(8,128)S(1)} %all_to_all.15.got_ref), custom_call_target="tpu_custom_call" | custom-call | bytes 163840 | tf_op jit(solution)/shard_map/pallas_call | solution.py:191
  13.2 14.0 %all-to-all-start.1 = ((f32[32,16,256]{2,1,0:T(8,128)}), f32[32,16,256]{2,1,0:T(8,128)S(1)}, u32[]{:S(2)}, u32[]{:S(2)}) async-start(f32[32,16,256]{2,1,0:T(8,128)} %shard_map.57), calls=%async_computation.1 | async-start | bytes 1048576 | tf_op jit(solution)/shard_map/all_to_all | solution.py:222
  27.2 1.9 %collective-permute-start = (f32[8,24,128]{2,1,0:T(8,128)S(1)}, f32[8,24,128]{2,1,0:T(8,128)S(1)}, u32[]{:S(2)}, u32[]{:S(2)}) collective-permute-start(f32[8,24,128]{2,1,0:T(8,128)S(1)} %slice.4.own_ref), channel_id=1, source_target_pairs={{0,1},{1,0},{2,3},{3,2},{4,5},{5,4},{6,7},{7,6},{8,9},{9,8},{10,11... | collective-permute-start | bytes 294920 | tf_op jit(solution)/shard_map/ppermute | solution.py:228
  29.1 1.3 %collective-permute-done.other_ref = f32[8,24,128]{2,1,0:T(8,128)S(1)} collective-permute-done((f32[8,24,128]{2,1,0:T(8,128)S(1)}, f32[8,24,128]{2,1,0:T(8,128)S(1)}, u32[]{:S(2)}, u32[]{:S(2)}) %collective-permute-start) | collective-permute-done | bytes 98336 | tf_op jit(solution)/shard_map/ppermute | solution.py:228
  30.4 0.2 shard_map.56
  30.6 13.2 %all-to-all-done.1.steps_ref = f32[32,16,256]{2,1,0:T(8,128)S(1)} async-done(((f32[32,16,256]{2,1,0:T(8,128)}), f32[32,16,256]{2,1,0:T(8,128)S(1)}, u32[]{:S(2)}, u32[]{:S(2)}) %all-to-all-start.1) | async-done | bytes 524320 | tf_op jit(solution)/shard_map/all_to_all | solution.py:222
  43.9 0.4 shard_map.58
  44.3 0.0 copy-start
  44.3 0.0 copy-start.1
  44.3 0.0 copy-start.2
  44.3 22.6 %all_to_all.16.got_ref = f32[16,48,128]{2,1,0:T(8,128)S(1)} all-to-all(f32[16,48,128]{2,1,0:T(8,128)S(1)} %shard_map.58), channel_id=1, replica_groups=mesh['z'=8,'yl'=4,'x'=4,'yh'=2,'c'=2] {'x','yh','c'}, dimensions={0} | all-to-all | bytes 786432 | tf_op jit(solution)/shard_map/all_to_all | solution.py:238
  66.9 0.0 copy-done
  66.9 0.0 copy-done.1
  66.9 0.0 copy-done.2
  66.9 1.3 %shard_map.59 = f32[384,128]{1,0:T(8,128)} custom-call(f32[16,48,128]{2,1,0:T(8,128)S(1)} %all_to_all.16.got_ref, bf16[256,512]{1,0:T(8,128)(2,1)S(1)} %copy-done.1, bf16[256,512]{1,0:T(8,128)(2,1)S(1)} %copy-done, f32[2,16,256]{2,1,0:T(8,128)S(1)} %copy-done.2), custom_call_target="tpu_custom_call" | custom-call | bytes 950272 | tf_op jit(solution)/shard_map/pallas_call | solution.py:191
  (1 shorter events, 0.0 us)
Async XLA Ops:
  13.2 30.6 %all-to-all-start.1 = ((f32[32,16,256]{2,1,0:T(8,128)}), f32[32,16,256]{2,1,0:T(8,128)S(1)}, u32[]{:S(2)}, u32[]{:S(2)}) async-start(f32[32,16,256]{2,1,0:T(8,128)} %shard_map.57), calls=%async_computation.1 | async-start | bytes 1048576 | tf_op jit(solution)/shard_map/all_to_all | solution.py:222
  27.2 3.2 %collective-permute-start = (f32[8,24,128]{2,1,0:T(8,128)S(1)}, f32[8,24,128]{2,1,0:T(8,128)S(1)}, u32[]{:S(2)}, u32[]{:S(2)}) collective-permute-start(f32[8,24,128]{2,1,0:T(8,128)S(1)} %slice.4.own_ref), channel_id=1, source_target_pairs={{0,1},{1,0},{2,3},{3,2},{4,5},{5,4},{6,7},{7,6},{8,9},{9,8},{10,11... | collective-permute-start | bytes 294920 | tf_op jit(solution)/shard_map/ppermute | solution.py:228
  44.3 22.7 %copy-start = (bf16[256,512]{1,0:T(8,128)(2,1)S(1)}, bf16[256,512]{1,0:T(8,128)(2,1)}, u32[]{:S(2)}) copy-start(bf16[256,512]{1,0:T(8,128)(2,1)} %constant.7.clone.low_ref) | copy-start | bytes 786436
  44.3 22.7 %copy-start.1 = (bf16[256,512]{1,0:T(8,128)(2,1)S(1)}, bf16[256,512]{1,0:T(8,128)(2,1)}, u32[]{:S(2)}) copy-start(bf16[256,512]{1,0:T(8,128)(2,1)} %constant.6.clone.high_ref) | copy-start | bytes 786436
  44.3 22.6 %copy-start.2 = (f32[2,16,256]{2,1,0:T(8,128)S(1)}, f32[2,16,256]{2,1,0:T(8,128)}, u32[]{:S(2)}) copy-start(f32[2,16,256]{2,1,0:T(8,128)} %constant.8.clone.twist_ref) | copy-start | bytes 98308

commit v5 on v4

--- a/solution.py
+++ b/solution.py
@@ -7,12 +7,14 @@
 from jax.experimental.pallas import tpu as pltpu
 from jax.sharding import Mesh, PartitionSpec as P
 
-PARTS = ("z", "yl", "x", "yh", "c")
-SIZES = (8, 4, 4, 2, 2)
-ELEM = ("z", "yl")
+PARTS = ("z", "ya", "yb", "x", "yh", "c")
+SIZES = (8, 2, 2, 4, 2, 2)
+ELEM = ("z", "ya", "yb")
 MODE = ("x", "yh", "c")
 PAIR = ("x", "c")
-BLOCKS, SHARES, PAIRS = 32, 16, 8
+PLANE = ("z", "ya")
+LAST = ("yh", "c", "x", "yb")
+BLOCKS, SHARES, PAIRS = 16, 16, 8
 STEPS, MODES = 4096, 256
 SLOW, FAST = 256, 16
 OWNED, PADDED = 12, 16
@@ -37,6 +39,8 @@
     k1 = np.arange(SLOW)
     angle = 2.0 * np.pi * ((k1[:, None] * k1[None, :]) % SLOW) / SLOW
     first = np.concatenate([np.cos(angle), -np.sin(angle)], axis=1) / np.sqrt(STEPS)
+    first = first.reshape(BLOCKS, 2, 8, 2 * SLOW).transpose(1, 0, 2, 3)
+    first = first.reshape(SLOW, 2 * SLOW)
     high = first.astype(np.float32).astype(jnp.bfloat16)
     low = (first - high.astype(np.float64)).astype(jnp.bfloat16)
     turn = 2.0 * np.pi * (np.arange(FAST)[:, None] * k1[None, :]) / STEPS
@@ -58,17 +62,15 @@
         copy.wait()
     tall[...] = wide[...].T
     half = modes // 2
+    rest = width - LANES
     for pair in range(PAIRS):
         for high in range(2):
             rows = tall[pl.ds(8 * high + pair, LANES // FAST, stride=FAST), :]
             out_ref[pair, pl.ds(high * 8, 8), :] = rows
-        first = (pair % 2) * half
-        out_ref[pair, pl.ds(16, half), :] = modes_ref[pl.ds(first, half), :LANES]
-        rest = width - LANES
+        out_ref[pair, pl.ds(16, modes), :] = modes_ref[:, :LANES]
         for side in range(2):
-            out_ref[pair, pl.ds(16 + half, 8), pl.ds(side * rest, rest)] = modes_ref[
-                pl.ds(first + side * 8, 8), LANES:
-            ]
+            to = (pair, pl.ds(16 + modes, half), pl.ds(side * rest, rest))
+            out_ref[to] = modes_ref[pl.ds(side * half, half), LANES:]
 
 
 def spread(got_ref, out_ref):
@@ -82,32 +84,41 @@
 
 
 def order_modes(own_ref, other_ref, high_ref, low_ref, whole):
-    c = lax.axis_index("c")
-    half = MODES // PAIRS // 2
-    rest = whole.shape[1] - LANES
-    for ref, which in ((own_ref, c), (other_ref, 1 - c)):
+    yb = lax.axis_index("yb")
+    modes = MODES // PAIRS
+    half = modes // 2
+    width = whole.shape[1]
+    rest = width - LANES
+    for ref, which in ((own_ref, yb), (other_ref, 1 - yb)):
         for sender in range(PAIRS):
-            at = pl.multiple_of(sender * 2 * half + which * half, half)
-            whole[pl.ds(at, half), pl.ds(0, LANES)] = ref[sender, pl.ds(0, half), :]
+            at = sender * modes
+            whole[pl.ds(at, modes), :LANES] = ref[sender, pl.ds(0, modes), :]
             for side in range(2):
-                rows = pl.ds(pl.multiple_of(at + side * 8, 8), 8)
-                whole[rows, pl.ds(LANES, rest)] = ref[
-                    sender, pl.ds(half, 8), pl.ds(side * rest, rest)
+                whole[pl.ds(at + side * half, half), LANES:] = ref[
+                    sender, pl.ds(modes, half), pl.ds(side * rest, rest)
                 ]
-    high_ref[...], low_ref[...] = split(whole[...].T)
+        to = (pl.ds(pl.multiple_of(which * width, width), width), slice(None))
+        high_ref[to], low_ref[to] = split(whole[...].T)
+
+
+def last_index(yh, c, x, yb):
+    return ((yh * 2 + c) * 4 + x) * 2 + yb
 
 
 def contract(high_ref, low_ref, steps_ref, out_ref):
-    modes = (high_ref[...], low_ref[...])
-    tiles = SLOW // LANES
-    for high in range(2):
-        steps = steps_ref[:, pl.ds(8 * high, 8), :].reshape(SLOW, MODES)
-        stress = product(modes, split(steps), NT)
-        for owner in range(SHARES):
-            for tile in range(tiles):
-                out_ref[owner, pl.ds((high * tiles + tile) * OWNED, OWNED), :] = stress[
-                    owner * OWNED : (owner + 1) * OWNED,
-                    tile * LANES : (tile + 1) * LANES,
+    steps = [
+        steps_ref[:, pl.ds(8 * high, 8), :].reshape(LANES, MODES) for high in range(2)
+    ]
+    stress = product(
+        (high_ref[...], low_ref[...]), split(jnp.concatenate(steps)), NT
+    )
+    for yb in range(2):
+        for share in range(SHARES):
+            owner = last_index(share // 2 % 2, share % 2, share // 4, yb)
+            first = (yb * SHARES + share) * OWNED
+            for high in range(2):
+                out_ref[owner, pl.ds(high * OWNED, OWNED), :] = stress[
+                    first : first + OWNED, high * LANES : (high + 1) * LANES
                 ]
 
 
@@ -150,11 +161,12 @@
 
 def spectra(got_ref, high_ref, low_ref, twist_ref, out_ref, rows_high, rows_low, stage):
     for n2 in range(FAST):
-        for tile in range(SLOW // LANES):
-            at = (pl.ds(n2 * PADDED, OWNED), pl.ds(tile * LANES, LANES))
-            sender = (n2 % 8) // 2 * 4 + n2 % 2
-            part = pl.ds((n2 // 8 * 2 + tile) * OWNED, OWNED)
-            value = got_ref[sender, part, :] + got_ref[sender + 2, part, :]
+        for yb in range(2):
+            at = (pl.ds(n2 * PADDED, OWNED), pl.ds(yb * LANES, LANES))
+            rows = pl.ds(n2 // 8 * OWNED, OWNED)
+            x, c = n2 % 8 // 2, n2 % 2
+            low = got_ref[last_index(0, c, x, yb), rows, :]
+            value = low + got_ref[last_index(1, c, x, yb), rows, :]
             rows_high[at], rows_low[at] = split(value)
     stage[...] = product(
         (rows_high[...], rows_low[...]), (high_ref[...], low_ref[...]), NN
@@ -209,7 +221,7 @@
     vmem = pltpu.VMEM
     sent = call(
         scatter,
-        shape((PAIRS, 16 + 24, LANES), f32),
+        shape((PAIRS, 16 + 48, LANES), f32),
         modal_history.T,
         stress_modes,
         scratch=[vmem((LANES, LANES), f32)] * 2
@@ -219,23 +231,23 @@
     )
     got = lax.all_to_all(sent, PAIR, split_axis=0, concat_axis=0, tiled=True)
     history = call(spread, shape((BLOCKS, 16, MODES), f32), got)
-    steps = lax.all_to_all(history, ELEM, split_axis=0, concat_axis=0, tiled=True)
+    steps = lax.all_to_all(history, PLANE, split_axis=0, concat_axis=0, tiled=True)
     own = got[:, 16:]
     high, low = call(
         order_modes,
-        (shape((width, MODES), bf16), shape((width, MODES), bf16)),
+        (shape((2 * width, MODES), bf16), shape((2 * width, MODES), bf16)),
         own,
-        lax.ppermute(own, "c", [(0, 1), (1, 0)]),
+        lax.ppermute(own, "yb", [(0, 1), (1, 0)]),
         scratch=[vmem((MODES, width), f32)],
     )
     stress = call(
         contract,
-        shape((SHARES, 2 * SLOW // LANES * OWNED, LANES), f32),
+        shape((2 * SHARES, 2 * OWNED, LANES), f32),
         high,
         low,
         steps,
     )
-    owned = lax.all_to_all(stress, MODE, split_axis=0, concat_axis=0, tiled=True)
+    owned = lax.all_to_all(stress, LAST, split_axis=0, concat_axis=0, tiled=True)
     first_high, first_low, twist = tables()
     rows = FAST * PADDED
     out = call(

time: 68.6 us -> 64.1 us (0.934)
  the two profiles are of different devices: /device:TPU:8 before, /device:TPU:1 now
where the time goes in v5:
time: 64.1 us; the launch traced here: 63.2 us
  blocking collectives  41.9 us (65%)
  starting transfers between devices  11 us (17%)
  waiting for transfers between devices  6.01 us (9%)
  Pallas kernels  4.21 us (7%)
    all_to_all x1, blocking collectives, per_device(): lax.all_to_all(stress, LAST, split_axis=0, concat_axis=0, tiled=True)  25.2 us
    all_to_all x1, blocking collectives, per_device(): got = lax.all_to_all(sent, PAIR, split_axis=0, concat_axis=0, tiled=True)  16.7 us
    all_to_all x1, starting transfers between devices, per_device(): lax.all_to_all(history, PLANE, split_axis=0, concat_axis=0, tiled=True)  7.78 us
    ppermute x1, waiting for transfers between devices, per_device(): lax.ppermute(own, 'yb', [(0, 1), (1, 0)])  5.66 us
    pallas_call x5, Pallas kernels, call(): pl.pallas_call(kernel, out_shape=shapes, in_specs=[pl.BlockSpec(memory_sp...  4.21 us
    ppermute x1, starting transfers between devices, per_device(): lax.ppermute(own, 'yb', [(0, 1), (1, 0)])  3.2 us
  transfers between devices with their start and end apart: 2, of which 2 were waited for; matrix products, arithmetic and copies ran while one was open for 0% of the time, Pallas kernels for 0%

profile of v5, /device:TPU:1, one launch (start us, length us, event | category | flops | bytes accessed | tf_op | source)
XLA Modules:
  0.0 63.2 jit_solution(1606820931887162587)
XLA Ops:
  0.0 1.6 %shard_map.55 = f32[8,64,128]{2,1,0:T(8,128)} custom-call(f32[32,128]{1,0:T(8,128)} %bitcast.6, f32[32,192]{1,0:T(8,128)} %modes_hbm.1), custom_call_target="tpu_custom_call" | custom-call | bytes 40960 | tf_op jit(solution)/shard_map/pallas_call | solution.py:203
  1.6 16.7 %all_to_all.15.got_ref = f32[8,64,128]{2,1,0:T(8,128)S(1)} all-to-all(f32[8,64,128]{2,1,0:T(8,128)} %shard_map.55), channel_id=1, replica_groups=mesh['z'=8,'ya'=2,'yb'=2,'x'=4,'yh'=2,'c'=2] {'x','c'}, dimensions={0} | all-to-all | bytes 524288 | tf_op jit(solution)/shard_map/all_to_all | solution.py:232
  18.3 0.7 %shard_map.57 = f32[16,16,256]{2,1,0:T(8,128)} custom-call(f32[8,64,128]{2,1,0:T(8,128)S(1)} %all_to_all.15.got_ref), custom_call_target="tpu_custom_call" | custom-call | bytes 262144 | tf_op jit(solution)/shard_map/pallas_call | solution.py:203
  19.1 7.8 %all-to-all-start.1 = ((f32[16,16,256]{2,1,0:T(8,128)}), f32[16,16,256]{2,1,0:T(8,128)S(1)}, u32[]{:S(2)}, u32[]{:S(2)}) async-start(f32[16,16,256]{2,1,0:T(8,128)} %shard_map.57), calls=%async_computation.1 | async-start | bytes 524288 | tf_op jit(solution)/shard_map/all_to_all | solution.py:234
  26.9 3.2 %collective-permute-start = (f32[8,48,128]{2,1,0:T(8,128)S(1)}, f32[8,48,128]{2,1,0:T(8,128)S(1)}, u32[]{:S(2)}, u32[]{:S(2)}) collective-permute-start(f32[8,48,128]{2,1,0:T(8,128)S(1)} %slice.4.own_ref), channel_id=1, source_target_pairs={{0,16},{16,0},{1,17},{17,1},{2,18},{18,2},{3,19},{19,3},{4,20},{20... | collective-permute-start | bytes 589832 | tf_op jit(solution)/shard_map/ppermute | solution.py:240
  30.1 5.7 %collective-permute-done.other_ref = f32[8,48,128]{2,1,0:T(8,128)S(1)} collective-permute-done((f32[8,48,128]{2,1,0:T(8,128)S(1)}, f32[8,48,128]{2,1,0:T(8,128)S(1)}, u32[]{:S(2)}, u32[]{:S(2)}) %collective-permute-start) | collective-permute-done | bytes 196640 | tf_op jit(solution)/shard_map/ppermute | solution.py:240
  35.7 0.3 shard_map.56
  36.0 0.4 all-to-all-done.1.steps_ref
  36.4 0.3 shard_map.58
  36.7 0.0 copy-start
  36.7 0.0 copy-start.1
  36.7 0.0 copy-start.2
  36.7 25.2 %all_to_all.16.got_ref = f32[32,24,128]{2,1,0:T(8,128)S(1)} all-to-all(f32[32,24,128]{2,1,0:T(8,128)S(1)} %shard_map.58), channel_id=1, replica_groups=mesh['z'=8,'ya'=2,'yb'=2,'x'=4,'yh'=2,'c'=2] {'yh','c','x','yb'}, dimensions={0} | all-to-all | bytes 786432 | tf_op jit(solution)/shard_map/all_to_all | solution.py:250
  62.0 0.0 copy-done
  62.0 0.0 copy-done.1
  62.0 0.0 copy-done.2
  62.0 1.3 %shard_map.59 = f32[384,128]{1,0:T(8,128)} custom-call(f32[32,24,128]{2,1,0:T(8,128)S(1)} %all_to_all.16.got_ref, bf16[256,512]{1,0:T(8,128)(2,1)S(1)} %copy-done.1, bf16[256,512]{1,0:T(8,128)(2,1)S(1)} %copy-done, f32[2,16,256]{2,1,0:T(8,128)S(1)} %copy-done.2), custom_call_target="tpu_custom_call" | custom-call | bytes 950272 | tf_op jit(solution)/shard_map/pallas_call | solution.py:203
  (1 shorter events, 0.0 us)
Async XLA Ops:
  19.1 17.3 %all-to-all-start.1 = ((f32[16,16,256]{2,1,0:T(8,128)}), f32[16,16,256]{2,1,0:T(8,128)S(1)}, u32[]{:S(2)}, u32[]{:S(2)}) async-start(f32[16,16,256]{2,1,0:T(8,128)} %shard_map.57), calls=%async_computation.1 | async-start | bytes 524288 | tf_op jit(solution)/shard_map/all_to_all | solution.py:234
  26.9 8.9 %collective-permute-start = (f32[8,48,128]{2,1,0:T(8,128)S(1)}, f32[8,48,128]{2,1,0:T(8,128)S(1)}, u32[]{:S(2)}, u32[]{:S(2)}) collective-permute-start(f32[8,48,128]{2,1,0:T(8,128)S(1)} %slice.4.own_ref), channel_id=1, source_target_pairs={{0,16},{16,0},{1,17},{17,1},{2,18},{18,2},{3,19},{19,3},{4,20},{20... | collective-permute-start | bytes 589832 | tf_op jit(solution)/shard_map/ppermute | solution.py:240
  36.7 25.3 %copy-start = (bf16[256,512]{1,0:T(8,128)(2,1)S(1)}, bf16[256,512]{1,0:T(8,128)(2,1)}, u32[]{:S(2)}) copy-start(bf16[256,512]{1,0:T(8,128)(2,1)} %constant.7.clone.low_ref) | copy-start | bytes 786436
  36.7 25.3 %copy-start.1 = (bf16[256,512]{1,0:T(8,128)(2,1)S(1)}, bf16[256,512]{1,0:T(8,128)(2,1)}, u32[]{:S(2)}) copy-start(bf16[256,512]{1,0:T(8,128)(2,1)} %constant.6.clone.high_ref) | copy-start | bytes 786436
  36.7 25.2 %copy-start.2 = (f32[2,16,256]{2,1,0:T(8,128)S(1)}, f32[2,16,256]{2,1,0:T(8,128)}, u32[]{:S(2)}) copy-start(f32[2,16,256]{2,1,0:T(8,128)} %constant.8.clone.twist_ref) | copy-start | bytes 98308

commit v6 on v5

--- a/solution.py
+++ b/solution.py
@@ -7,13 +7,14 @@
 from jax.experimental.pallas import tpu as pltpu
 from jax.sharding import Mesh, PartitionSpec as P
 
-PARTS = ("z", "ya", "yb", "x", "yh", "c")
-SIZES = (8, 2, 2, 4, 2, 2)
-ELEM = ("z", "ya", "yb")
-MODE = ("x", "yh", "c")
-PAIR = ("x", "c")
-PLANE = ("z", "ya")
-LAST = ("yh", "c", "x", "yb")
+PARTS = ("z2", "z1", "z0", "y1", "y0", "x1", "x0", "y2", "c")
+SIZES = (2,) * 9
+ELEM = ("z2", "z1", "z0", "y1", "y0")
+MODE = ("x1", "x0", "y2", "c")
+PAIR = ("x1", "x0", "c")
+PLANE = ("y1", "z2", "z1", "z0")
+SIDE = "y0"
+LAST = ("y2", "y0", "c", "x1", "x0")
 BLOCKS, SHARES, PAIRS = 16, 16, 8
 STEPS, MODES = 4096, 256
 SLOW, FAST = 256, 16
@@ -39,8 +40,11 @@
     k1 = np.arange(SLOW)
     angle = 2.0 * np.pi * ((k1[:, None] * k1[None, :]) % SLOW) / SLOW
     first = np.concatenate([np.cos(angle), -np.sin(angle)], axis=1) / np.sqrt(STEPS)
-    first = first.reshape(BLOCKS, 2, 8, 2 * SLOW).transpose(1, 0, 2, 3)
-    first = first.reshape(SLOW, 2 * SLOW)
+    first = first.reshape(2 * BLOCKS, 8, 2 * SLOW)
+    order = [
+        index_of(ELEM, **{SIDE: side}, **place) for side in range(2) for place in places(PLANE)
+    ]
+    first = first[np.array(order)].reshape(SLOW, 2 * SLOW)
     high = first.astype(np.float32).astype(jnp.bfloat16)
     low = (first - high.astype(np.float64)).astype(jnp.bfloat16)
     turn = 2.0 * np.pi * (np.arange(FAST)[:, None] * k1[None, :]) / STEPS
@@ -68,9 +72,9 @@
             rows = tall[pl.ds(8 * high + pair, LANES // FAST, stride=FAST), :]
             out_ref[pair, pl.ds(high * 8, 8), :] = rows
         out_ref[pair, pl.ds(16, modes), :] = modes_ref[:, :LANES]
-        for side in range(2):
-            to = (pair, pl.ds(16 + modes, half), pl.ds(side * rest, rest))
-            out_ref[to] = modes_ref[pl.ds(side * half, half), LANES:]
+        for part in range(2):
+            to = (pair, pl.ds(16 + modes, half), pl.ds(part * rest, rest))
+            out_ref[to] = modes_ref[pl.ds(part * half, half), LANES:]
 
 
 def spread(got_ref, out_ref):
@@ -84,25 +88,34 @@
 
 
 def order_modes(own_ref, other_ref, high_ref, low_ref, whole):
-    yb = lax.axis_index("yb")
+    side = lax.axis_index(SIDE)
     modes = MODES // PAIRS
     half = modes // 2
     width = whole.shape[1]
     rest = width - LANES
-    for ref, which in ((own_ref, yb), (other_ref, 1 - yb)):
+    for ref, which in ((own_ref, side), (other_ref, 1 - side)):
         for sender in range(PAIRS):
             at = sender * modes
             whole[pl.ds(at, modes), :LANES] = ref[sender, pl.ds(0, modes), :]
-            for side in range(2):
-                whole[pl.ds(at + side * half, half), LANES:] = ref[
-                    sender, pl.ds(modes, half), pl.ds(side * rest, rest)
+            for part in range(2):
+                whole[pl.ds(at + part * half, half), LANES:] = ref[
+                    sender, pl.ds(modes, half), pl.ds(part * rest, rest)
                 ]
         to = (pl.ds(pl.multiple_of(which * width, width), width), slice(None))
         high_ref[to], low_ref[to] = split(whole[...].T)
 
 
-def last_index(yh, c, x, yb):
-    return ((yh * 2 + c) * 4 + x) * 2 + yb
+def index_of(axes, **at):
+    index = 0
+    for axis in axes:
+        index = index * dict(zip(PARTS, SIZES))[axis] + at[axis]
+    return index
+
+
+def places(axes):
+    sizes = dict(zip(PARTS, SIZES))
+    grid = np.indices([sizes[a] for a in axes]).reshape(len(axes), -1)
+    return [dict(zip(axes, map(int, column))) for column in grid.T]
 
 
 def contract(high_ref, low_ref, steps_ref, out_ref):
@@ -112,10 +125,10 @@
     stress = product(
         (high_ref[...], low_ref[...]), split(jnp.concatenate(steps)), NT
     )
-    for yb in range(2):
+    for side in range(2):
         for share in range(SHARES):
-            owner = last_index(share // 2 % 2, share % 2, share // 4, yb)
-            first = (yb * SHARES + share) * OWNED
+            owner = index_of(LAST, **{SIDE: side}, **places(MODE)[share])
+            first = (side * SHARES + share) * OWNED
             for high in range(2):
                 out_ref[owner, pl.ds(high * OWNED, OWNED), :] = stress[
                     first : first + OWNED, high * LANES : (high + 1) * LANES
@@ -161,12 +174,12 @@
 
 def spectra(got_ref, high_ref, low_ref, twist_ref, out_ref, rows_high, rows_low, stage):
     for n2 in range(FAST):
-        for yb in range(2):
-            at = (pl.ds(n2 * PADDED, OWNED), pl.ds(yb * LANES, LANES))
+        for side in range(2):
+            at = (pl.ds(n2 * PADDED, OWNED), pl.ds(side * LANES, LANES))
             rows = pl.ds(n2 // 8 * OWNED, OWNED)
-            x, c = n2 % 8 // 2, n2 % 2
-            low = got_ref[last_index(0, c, x, yb), rows, :]
-            value = low + got_ref[last_index(1, c, x, yb), rows, :]
+            place = places(PAIR)[n2 % 8]
+            senders = [index_of(LAST, **{SIDE: side}, y2=y2, **place) for y2 in range(2)]
+            value = got_ref[senders[0], rows, :] + got_ref[senders[1], rows, :]
             rows_high[at], rows_low[at] = split(value)
     stage[...] = product(
         (rows_high[...], rows_low[...]), (high_ref[...], low_ref[...]), NN
@@ -237,7 +250,7 @@
         order_modes,
         (shape((2 * width, MODES), bf16), shape((2 * width, MODES), bf16)),
         own,
-        lax.ppermute(own, "yb", [(0, 1), (1, 0)]),
+        lax.ppermute(own, SIDE, [(0, 1), (1, 0)]),
         scratch=[vmem((MODES, width), f32)],
     )
     stress = call(

time: 64.1 us -> 62.5 us (0.975)
  blocking collectives: 41.9 us -> 40.3 us
    all_to_all x1, blocking collectives: 25.2 us -> 23.6 us  [per_device(): lax.all_to_all(stress, LAST, split_axis=0, concat_axis=0, tiled=True)]
where the time goes in v6:
time: 62.5 us; the launch traced here: 61.8 us
  blocking collectives  40.3 us (64%)
  starting transfers between devices  11 us (18%)
  waiting for transfers between devices  6.31 us (10%)
  Pallas kernels  4.19 us (7%)
    all_to_all x1, blocking collectives, per_device(): lax.all_to_all(stress, LAST, split_axis=0, concat_axis=0, tiled=True)  23.6 us
    all_to_all x1, blocking collectives, per_device(): got = lax.all_to_all(sent, PAIR, split_axis=0, concat_axis=0, tiled=True)  16.7 us
    all_to_all x1, starting transfers between devices, per_device(): lax.all_to_all(history, PLANE, split_axis=0, concat_axis=0, tiled=True)  7.78 us
    ppermute x1, waiting for transfers between devices, per_device(): lax.ppermute(own, SIDE, [(0, 1), (1, 0)])  5.66 us
    pallas_call x5, Pallas kernels, call(): pl.pallas_call(kernel, out_shape=shapes, in_specs=[pl.BlockSpec(memory_sp...  4.19 us
    ppermute x1, starting transfers between devices, per_device(): lax.ppermute(own, SIDE, [(0, 1), (1, 0)])  3.2 us
  transfers between devices with their start and end apart: 2, of which 2 were waited for; matrix products, arithmetic and copies ran while one was open for 0% of the time, Pallas kernels for 0%

profile of v6, /device:TPU:1, one launch (start us, length us, event | category | flops | bytes accessed | tf_op | source)
XLA Modules:
  0.0 61.8 jit_solution(17887391341898087025)
XLA Ops:
  0.0 1.6 %shard_map.55 = f32[8,64,128]{2,1,0:T(8,128)} custom-call(f32[32,128]{1,0:T(8,128)} %bitcast.6, f32[32,192]{1,0:T(8,128)} %modes_hbm.1), custom_call_target="tpu_custom_call" | custom-call | bytes 40960 | tf_op jit(solution)/shard_map/pallas_call | solution.py:216
  1.6 16.7 %all_to_all.15.got_ref = f32[8,64,128]{2,1,0:T(8,128)S(1)} all-to-all(f32[8,64,128]{2,1,0:T(8,128)} %shard_map.55), channel_id=1, replica_groups=mesh['z2'=2,'z1'=2,'z0'=2,'y1'=2,'y0'=2,'x1'=2,'x0'=2,'y2'=2,'c'=2] {'x1..., dimensions={0} | all-to-all | bytes 524288 | tf_op jit(solution)/shard_map/all_to_all | solution.py:245
  18.3 0.7 %shard_map.57 = f32[16,16,256]{2,1,0:T(8,128)} custom-call(f32[8,64,128]{2,1,0:T(8,128)S(1)} %all_to_all.15.got_ref), custom_call_target="tpu_custom_call" | custom-call | bytes 262144 | tf_op jit(solution)/shard_map/pallas_call | solution.py:216
  19.1 7.8 %all-to-all-start.1 = ((f32[16,16,256]{2,1,0:T(8,128)}), f32[16,16,256]{2,1,0:T(8,128)S(1)}, u32[]{:S(2)}, u32[]{:S(2)}) async-start(f32[16,16,256]{2,1,0:T(8,128)} %shard_map.57), calls=%async_computation.1 | async-start | bytes 524288 | tf_op jit(solution)/shard_map/all_to_all | solution.py:247
  26.9 3.2 %collective-permute-start = (f32[8,48,128]{2,1,0:T(8,128)S(1)}, f32[8,48,128]{2,1,0:T(8,128)S(1)}, u32[]{:S(2)}, u32[]{:S(2)}) collective-permute-start(f32[8,48,128]{2,1,0:T(8,128)S(1)} %slice.4.own_ref), channel_id=1, source_target_pairs={{0,16},{16,0},{1,17},{17,1},{2,18},{18,2},{3,19},{19,3},{4,20},{20... | collective-permute-start | bytes 589832 | tf_op jit(solution)/shard_map/ppermute | solution.py:253
  30.1 5.7 %collective-permute-done.other_ref = f32[8,48,128]{2,1,0:T(8,128)S(1)} collective-permute-done((f32[8,48,128]{2,1,0:T(8,128)S(1)}, f32[8,48,128]{2,1,0:T(8,128)S(1)}, u32[]{:S(2)}, u32[]{:S(2)}) %collective-permute-start) | collective-permute-done | bytes 196640 | tf_op jit(solution)/shard_map/ppermute | solution.py:253
  35.7 0.3 shard_map.56
  36.0 0.7 %all-to-all-done.1.steps_ref = f32[16,16,256]{2,1,0:T(8,128)S(1)} async-done(((f32[16,16,256]{2,1,0:T(8,128)}), f32[16,16,256]{2,1,0:T(8,128)S(1)}, u32[]{:S(2)}, u32[]{:S(2)}) %all-to-all-start.1) | async-done | bytes 262176 | tf_op jit(solution)/shard_map/all_to_all | solution.py:247
  36.6 0.3 shard_map.58
  37.0 0.0 copy-start
  37.0 0.0 copy-start.1
  37.0 0.0 copy-start.2
  37.0 23.6 %all_to_all.16.got_ref = f32[32,24,128]{2,1,0:T(8,128)S(1)} all-to-all(f32[32,24,128]{2,1,0:T(8,128)S(1)} %shard_map.58), channel_id=1, replica_groups=mesh['z2'=2,'z1'=2,'z0'=2,'y1'=2,'y0'=2,'x1'=2,'x0'=2,'y2'=2,'c'=2] {'y2..., dimensions={0} | all-to-all | bytes 786432 | tf_op jit(solution)/shard_map/all_to_all | solution.py:263
  60.6 0.0 copy-done
  60.6 0.0 copy-done.1
  60.6 0.0 copy-done.2
  60.6 1.2 %shard_map.59 = f32[384,128]{1,0:T(8,128)} custom-call(f32[32,24,128]{2,1,0:T(8,128)S(1)} %all_to_all.16.got_ref, bf16[256,512]{1,0:T(8,128)(2,1)S(1)} %copy-done.1, bf16[256,512]{1,0:T(8,128)(2,1)S(1)} %copy-done, f32[2,16,256]{2,1,0:T(8,128)S(1)} %copy-done.2), custom_call_target="tpu_custom_call" | custom-call | bytes 950272 | tf_op jit(solution)/shard_map/pallas_call | solution.py:216
  (1 shorter events, 0.0 us)
Async XLA Ops:
  19.1 17.6 %all-to-all-start.1 = ((f32[16,16,256]{2,1,0:T(8,128)}), f32[16,16,256]{2,1,0:T(8,128)S(1)}, u32[]{:S(2)}, u32[]{:S(2)}) async-start(f32[16,16,256]{2,1,0:T(8,128)} %shard_map.57), calls=%async_computation.1 | async-start | bytes 524288 | tf_op jit(solution)/shard_map/all_to_all | solution.py:247
  26.9 8.9 %collective-permute-start = (f32[8,48,128]{2,1,0:T(8,128)S(1)}, f32[8,48,128]{2,1,0:T(8,128)S(1)}, u32[]{:S(2)}, u32[]{:S(2)}) collective-permute-start(f32[8,48,128]{2,1,0:T(8,128)S(1)} %slice.4.own_ref), channel_id=1, source_target_pairs={{0,16},{16,0},{1,17},{17,1},{2,18},{18,2},{3,19},{19,3},{4,20},{20... | collective-permute-start | bytes 589832 | tf_op jit(solution)/shard_map/ppermute | solution.py:253
  37.0 23.6 %copy-start = (bf16[256,512]{1,0:T(8,128)(2,1)S(1)}, bf16[256,512]{1,0:T(8,128)(2,1)}, u32[]{:S(2)}) copy-start(bf16[256,512]{1,0:T(8,128)(2,1)} %constant.7.clone.low_ref) | copy-start | bytes 786436
  37.0 23.6 %copy-start.1 = (bf16[256,512]{1,0:T(8,128)(2,1)S(1)}, bf16[256,512]{1,0:T(8,128)(2,1)}, u32[]{:S(2)}) copy-start(bf16[256,512]{1,0:T(8,128)(2,1)} %constant.6.clone.high_ref) | copy-start | bytes 786436
  37.0 23.6 %copy-start.2 = (f32[2,16,256]{2,1,0:T(8,128)S(1)}, f32[2,16,256]{2,1,0:T(8,128)}, u32[]{:S(2)}) copy-start(f32[2,16,256]{2,1,0:T(8,128)} %constant.8.clone.twist_ref) | copy-start | bytes 98308

commit v7 on v6

--- a/solution.py
+++ b/solution.py
@@ -52,18 +52,12 @@
     return high, low, twist.astype(np.float32)
 
 
-def scatter(history_hbm, modes_hbm, out_ref, wide, tall, modes_ref, arrived):
-    modes, width = modes_ref.shape
+def scatter(both_ref, out_ref, wide, tall):
+    modes = both_ref.shape[0]
+    width = both_ref.shape[1] - LANES
     wide[...] = jnp.zeros_like(wide)
     at = pl.multiple_of(lax.rem(lax.axis_index(PAIR), LANES // modes) * modes, modes)
-    copies = (
-        pltpu.make_async_copy(history_hbm, wide.at[pl.ds(at, modes), :], arrived.at[0]),
-        pltpu.make_async_copy(modes_hbm, modes_ref, arrived.at[1]),
-    )
-    for copy in copies:
-        copy.start()
-    for copy in copies:
-        copy.wait()
+    wide[pl.ds(at, modes), :] = both_ref[:, :LANES]
     tall[...] = wide[...].T
     half = modes // 2
     rest = width - LANES
@@ -71,10 +65,10 @@
         for high in range(2):
             rows = tall[pl.ds(8 * high + pair, LANES // FAST, stride=FAST), :]
             out_ref[pair, pl.ds(high * 8, 8), :] = rows
-        out_ref[pair, pl.ds(16, modes), :] = modes_ref[:, :LANES]
+        out_ref[pair, pl.ds(16, modes), :] = both_ref[:, LANES : 2 * LANES]
         for part in range(2):
             to = (pair, pl.ds(16 + modes, half), pl.ds(part * rest, rest))
-            out_ref[to] = modes_ref[pl.ds(part * half, half), LANES:]
+            out_ref[to] = both_ref[pl.ds(part * half, half), 2 * LANES :]
 
 
 def spread(got_ref, out_ref):
@@ -235,12 +229,8 @@
     sent = call(
         scatter,
         shape((PAIRS, 16 + 48, LANES), f32),
-        modal_history.T,
-        stress_modes,
-        scratch=[vmem((LANES, LANES), f32)] * 2
-        + [vmem((modes, width), f32), pltpu.SemaphoreType.DMA((2,))],
-        space=pltpu.HBM,
-        limit=60 << 20,
+        jnp.concatenate([modal_history.T, stress_modes], axis=1),
+        scratch=[vmem((LANES, LANES), f32)] * 2,
     )
     got = lax.all_to_all(sent, PAIR, split_axis=0, concat_axis=0, tiled=True)
     history = call(spread, shape((BLOCKS, 16, MODES), f32), got)

time: 62.5 us -> 61.5 us (0.984)
  Pallas kernels: 4.19 us -> 2.72 us
  blocking collectives: 40.3 us -> 39.3 us
  other arithmetic: 0 us -> 0.77 us
  starting transfers between devices: 11 us -> 11.7 us
    pallas_call x5, Pallas kernels: 4.19 us -> 2.72 us  [call(): pl.pallas_call(kernel, out_shape=shapes, in_specs=[pl.BlockSpec(memory_sp...]
    all_to_all x1, blocking collectives: 16.7 us -> 15.8 us  [per_device(): got = lax.all_to_all(sent, PAIR, split_axis=0, concat_axis=0, tiled=True)]
    concatenate x0 -> x1, other arithmetic: none -> 0.77 us  [per_device(): jnp.concatenate([modal_history.T, stress_modes], axis=1)]
    all_to_all x1, starting transfers between devices: 7.78 us -> 8.48 us  [per_device(): lax.all_to_all(history, PLANE, split_axis=0, concat_axis=0, tiled=True)]
where the time goes in v7:
time: 61.5 us; the launch traced here: 60.9 us
  blocking collectives  39.3 us (64%)
  starting transfers between devices  11.7 us (19%)
  waiting for transfers between devices  6.31 us (10%)
  Pallas kernels  2.72 us (4%)
  other arithmetic  0.77 us (1%)
    all_to_all x1, blocking collectives, per_device(): lax.all_to_all(stress, LAST, split_axis=0, concat_axis=0, tiled=True)  23.6 us
    all_to_all x1, blocking collectives, per_device(): got = lax.all_to_all(sent, PAIR, split_axis=0, concat_axis=0, tiled=True)  15.8 us
    all_to_all x1, starting transfers between devices, per_device(): lax.all_to_all(history, PLANE, split_axis=0, concat_axis=0, tiled=True)  8.48 us
    ppermute x1, waiting for transfers between devices, per_device(): lax.ppermute(own, SIDE, [(0, 1), (1, 0)])  5.66 us
    ppermute x1, starting transfers between devices, per_device(): lax.ppermute(own, SIDE, [(0, 1), (1, 0)])  3.2 us
    pallas_call x5, Pallas kernels, call(): pl.pallas_call(kernel, out_shape=shapes, in_specs=[pl.BlockSpec(memory_sp...  2.72 us
  transfers between devices with their start and end apart: 2, of which 2 were waited for; matrix products, arithmetic and copies ran while one was open for 0% of the time, Pallas kernels for 0%

profile of v7, /device:TPU:1, one launch (start us, length us, event | category | flops | bytes accessed | tf_op | source)
XLA Modules:
  0.0 60.9 jit_solution(15220343394125096677)
XLA Ops:
  0.0 0.8 %pad_maximum_fusion.both_ref = f32[32,320]{1,0:T(8,128)S(1)} fusion(f32[32,192]{1,0:T(8,128)} %param.6, f32[32,128]{1,0:T(8,128)} %bitcast.6), kind=kLoop, calls=%fused_computation | loop fusion | flops 10240 | bytes 81920 | tf_op jit(solution)/shard_map/concatenate | solution.py:232
  0.8 0.1 shard_map.55
  0.9 15.8 %all_to_all.15.got_ref = f32[8,64,128]{2,1,0:T(8,128)S(1)} all-to-all(f32[8,64,128]{2,1,0:T(8,128)S(1)} %shard_map.55), channel_id=1, replica_groups=mesh['z2'=2,'z1'=2,'z0'=2,'y1'=2,'y0'=2,'x1'=2,'x0'=2,'y2'=2,'c'=2] {'x1..., dimensions={0} | all-to-all | bytes 524288 | tf_op jit(solution)/shard_map/all_to_all | solution.py:235
  16.7 0.7 %shard_map.57 = f32[16,16,256]{2,1,0:T(8,128)} custom-call(f32[8,64,128]{2,1,0:T(8,128)S(1)} %all_to_all.15.got_ref), custom_call_target="tpu_custom_call" | custom-call | bytes 262144 | tf_op jit(solution)/shard_map/pallas_call | solution.py:210
  17.4 8.5 %all-to-all-start.1 = ((f32[16,16,256]{2,1,0:T(8,128)}), f32[16,16,256]{2,1,0:T(8,128)S(1)}, u32[]{:S(2)}, u32[]{:S(2)}) async-start(f32[16,16,256]{2,1,0:T(8,128)} %shard_map.57), calls=%async_computation.1 | async-start | bytes 524288 | tf_op jit(solution)/shard_map/all_to_all | solution.py:237
  25.9 3.2 %collective-permute-start = (f32[8,48,128]{2,1,0:T(8,128)S(1)}, f32[8,48,128]{2,1,0:T(8,128)S(1)}, u32[]{:S(2)}, u32[]{:S(2)}) collective-permute-start(f32[8,48,128]{2,1,0:T(8,128)S(1)} %slice.4.own_ref), channel_id=1, source_target_pairs={{0,16},{16,0},{1,17},{17,1},{2,18},{18,2},{3,19},{19,3},{4,20},{20... | collective-permute-start | bytes 589832 | tf_op jit(solution)/shard_map/ppermute | solution.py:243
  29.2 5.7 %collective-permute-done.other_ref = f32[8,48,128]{2,1,0:T(8,128)S(1)} collective-permute-done((f32[8,48,128]{2,1,0:T(8,128)S(1)}, f32[8,48,128]{2,1,0:T(8,128)S(1)}, u32[]{:S(2)}, u32[]{:S(2)}) %collective-permute-start) | collective-permute-done | bytes 196640 | tf_op jit(solution)/shard_map/ppermute | solution.py:243
  34.8 0.3 shard_map.56
  35.1 0.7 %all-to-all-done.1.steps_ref = f32[16,16,256]{2,1,0:T(8,128)S(1)} async-done(((f32[16,16,256]{2,1,0:T(8,128)}), f32[16,16,256]{2,1,0:T(8,128)S(1)}, u32[]{:S(2)}, u32[]{:S(2)}) %all-to-all-start.1) | async-done | bytes 262176 | tf_op jit(solution)/shard_map/all_to_all | solution.py:237
  35.7 0.4 shard_map.58
  36.1 0.0 copy-start
  36.1 0.0 copy-start.1
  36.1 0.0 copy-start.2
  36.1 23.6 %all_to_all.16.got_ref = f32[32,24,128]{2,1,0:T(8,128)S(1)} all-to-all(f32[32,24,128]{2,1,0:T(8,128)S(1)} %shard_map.58), channel_id=1, replica_groups=mesh['z2'=2,'z1'=2,'z0'=2,'y1'=2,'y0'=2,'x1'=2,'x0'=2,'y2'=2,'c'=2] {'y2..., dimensions={0} | all-to-all | bytes 786432 | tf_op jit(solution)/shard_map/all_to_all | solution.py:253
  59.7 0.0 copy-done
  59.7 0.0 copy-done.1
  59.7 0.0 copy-done.2
  59.7 1.2 %shard_map.59 = f32[384,128]{1,0:T(8,128)} custom-call(f32[32,24,128]{2,1,0:T(8,128)S(1)} %all_to_all.16.got_ref, bf16[256,512]{1,0:T(8,128)(2,1)S(1)} %copy-done.1, bf16[256,512]{1,0:T(8,128)(2,1)S(1)} %copy-done, f32[2,16,256]{2,1,0:T(8,128)S(1)} %copy-done.2), custom_call_target="tpu_custom_call" | custom-call | bytes 950272 | tf_op jit(solution)/shard_map/pallas_call | solution.py:210
  (1 shorter events, 0.0 us)
Async XLA Ops:
  17.4 18.3 %all-to-all-start.1 = ((f32[16,16,256]{2,1,0:T(8,128)}), f32[16,16,256]{2,1,0:T(8,128)S(1)}, u32[]{:S(2)}, u32[]{:S(2)}) async-start(f32[16,16,256]{2,1,0:T(8,128)} %shard_map.57), calls=%async_computation.1 | async-start | bytes 524288 | tf_op jit(solution)/shard_map/all_to_all | solution.py:237
  25.9 8.9 %collective-permute-start = (f32[8,48,128]{2,1,0:T(8,128)S(1)}, f32[8,48,128]{2,1,0:T(8,128)S(1)}, u32[]{:S(2)}, u32[]{:S(2)}) collective-permute-start(f32[8,48,128]{2,1,0:T(8,128)S(1)} %slice.4.own_ref), channel_id=1, source_target_pairs={{0,16},{16,0},{1,17},{17,1},{2,18},{18,2},{3,19},{19,3},{4,20},{20... | collective-permute-start | bytes 589832 | tf_op jit(solution)/shard_map/ppermute | solution.py:243
  36.1 23.6 %copy-start = (bf16[256,512]{1,0:T(8,128)(2,1)S(1)}, bf16[256,512]{1,0:T(8,128)(2,1)}, u32[]{:S(2)}) copy-start(bf16[256,512]{1,0:T(8,128)(2,1)} %constant.7.clone.low_ref) | copy-start | bytes 786436
  36.1 23.6 %copy-start.1 = (bf16[256,512]{1,0:T(8,128)(2,1)S(1)}, bf16[256,512]{1,0:T(8,128)(2,1)}, u32[]{:S(2)}) copy-start(bf16[256,512]{1,0:T(8,128)(2,1)} %constant.6.clone.high_ref) | copy-start | bytes 786436
  36.1 23.6 %copy-start.2 = (f32[2,16,256]{2,1,0:T(8,128)S(1)}, f32[2,16,256]{2,1,0:T(8,128)}, u32[]{:S(2)}) copy-start(f32[2,16,256]{2,1,0:T(8,128)} %constant.8.clone.twist_ref) | copy-start | bytes 98308

commit v8 on v7

--- a/solution.py
+++ b/solution.py
@@ -56,45 +56,64 @@
     modes = both_ref.shape[0]
     width = both_ref.shape[1] - LANES
     wide[...] = jnp.zeros_like(wide)
-    at = pl.multiple_of(lax.rem(lax.axis_index(PAIR), LANES // modes) * modes, modes)
-    wide[pl.ds(at, modes), :] = both_ref[:, :LANES]
+    wide[pl.ds(0, modes), :] = both_ref[:, :LANES]
     tall[...] = wide[...].T
+    turn = lax.rem(lax.axis_index(PAIR), 4)
     half = modes // 2
     rest = width - LANES
+    turns = [lax.rem(quarter + turn, 4) * modes for quarter in range(4)]
     for pair in range(PAIRS):
-        for high in range(2):
-            rows = tall[pl.ds(8 * high + pair, LANES // FAST, stride=FAST), :]
-            out_ref[pair, pl.ds(high * 8, 8), :] = rows
-        out_ref[pair, pl.ds(16, modes), :] = both_ref[:, LANES : 2 * LANES]
+        first = pair % 2 * half
+        out_ref[pair, pl.ds(0, half), :] = both_ref[pl.ds(first, half), LANES : 2 * LANES]
         for part in range(2):
-            to = (pair, pl.ds(16 + modes, half), pl.ds(part * rest, rest))
-            out_ref[to] = both_ref[pl.ds(part * half, half), 2 * LANES :]
+            to = (pair, pl.ds(half, half // 2), pl.ds(part * rest, rest))
+            from_rows = pl.ds(first + part * (half // 2), half // 2)
+            out_ref[to] = both_ref[from_rows, 2 * LANES :]
+        joined = None
+        for quarter in range(4):
+            first = 8 * (quarter // 2) + pair + 4 * (quarter % 2) * FAST
+            rows = tall[pl.ds(first, 4, stride=FAST), :]
+            rows = pltpu.roll(rows, turns[quarter], 1)
+            joined = rows if joined is None else joined + rows
+        out_ref[pair, pl.ds(modes * 3 // 4, 4), :] = joined
 
 
 def spread(got_ref, out_ref):
+    lane = lax.broadcasted_iota(jnp.int32, (4, LANES), 1) // (LANES // 4)
     for quad in range(PAIRS // 4):
-        joined = None
-        for sender in range(4 * quad, 4 * quad + 4):
-            rows = got_ref[sender, pl.ds(0, 16), :]
-            joined = rows if joined is None else joined + rows
+        senders = [got_ref[4 * quad + k, pl.ds(24, 4), :] for k in range(4)]
+        quarters = []
+        for quarter in range(4):
+            value = senders[-quarter % 4]
+            for k in range(1, 4):
+                value = jnp.where(lane == k, senders[(k - quarter) % 4], value)
+            if quarter:
+                value = pltpu.roll(value, LANES - quarter * LANES // 4, 1)
+            quarters.append(value)
+        joined = jnp.concatenate(quarters)
         lanes = pl.ds(quad * LANES, LANES)
         out_ref[:, :, lanes] = jnp.broadcast_to(joined, (BLOCKS,) + joined.shape)
 
 
-def order_modes(own_ref, other_ref, high_ref, low_ref, whole):
-    side = lax.axis_index(SIDE)
+def order_modes(own_ref, core_ref, side_ref, both_ref, high_ref, low_ref, whole):
+    side, core = lax.axis_index(SIDE), lax.axis_index("c")
     modes = MODES // PAIRS
     half = modes // 2
     width = whole.shape[1]
     rest = width - LANES
-    for ref, which in ((own_ref, side), (other_ref, 1 - side)):
-        for sender in range(PAIRS):
-            at = sender * modes
-            whole[pl.ds(at, modes), :LANES] = ref[sender, pl.ds(0, modes), :]
-            for part in range(2):
-                whole[pl.ds(at + part * half, half), LANES:] = ref[
-                    sender, pl.ds(modes, half), pl.ds(part * rest, rest)
-                ]
+    for refs, which in (
+        ((own_ref, core_ref), side),
+        ((side_ref, both_ref), 1 - side),
+    ):
+        for ref, upper in zip(refs, (core, 1 - core)):
+            for sender in range(PAIRS):
+                at = pl.multiple_of(sender * modes + upper * half, half)
+                whole[pl.ds(at, half), :LANES] = ref[sender, pl.ds(0, half), :]
+                for part in range(2):
+                    rows = pl.ds(pl.multiple_of(at + part * (half // 2), 8), half // 2)
+                    whole[rows, LANES:] = ref[
+                        sender, pl.ds(half, half // 2), pl.ds(part * rest, rest)
+                    ]
         to = (pl.ds(pl.multiple_of(which * width, width), width), slice(None))
         high_ref[to], low_ref[to] = split(whole[...].T)
 
@@ -228,19 +247,24 @@
     vmem = pltpu.VMEM
     sent = call(
         scatter,
-        shape((PAIRS, 16 + 48, LANES), f32),
+        shape((PAIRS, 24 + 4, LANES), f32),
         jnp.concatenate([modal_history.T, stress_modes], axis=1),
         scratch=[vmem((LANES, LANES), f32)] * 2,
     )
     got = lax.all_to_all(sent, PAIR, split_axis=0, concat_axis=0, tiled=True)
     history = call(spread, shape((BLOCKS, 16, MODES), f32), got)
     steps = lax.all_to_all(history, PLANE, split_axis=0, concat_axis=0, tiled=True)
-    own = got[:, 16:]
+    own = got[:, :24]
+    core = lax.ppermute(own, "c", [(0, 1), (1, 0)])
+    side = lax.ppermute(own, SIDE, [(0, 1), (1, 0)])
+    both = lax.ppermute(own, (SIDE, "c"), [(i, i ^ 3) for i in range(4)])
     high, low = call(
         order_modes,
         (shape((2 * width, MODES), bf16), shape((2 * width, MODES), bf16)),
         own,
-        lax.ppermute(own, SIDE, [(0, 1), (1, 0)]),
+        core,
+        side,
+        both,
         scratch=[vmem((MODES, width), f32)],
     )
     stress = call(

time: 61.5 us -> 61.1 us (level)
  starting transfers between devices: 11.7 us -> 17 us
  waiting for transfers between devices: 6.31 us -> 3.06 us
  blocking collectives: 39.3 us -> 36.5 us
    ppermute x1 -> x3, starting transfers between devices: 3.2 us -> 8.46 us  [the longest x1 4.24 us: per_device(): both = lax.ppermute(own, (SIDE, 'c'), [(i, i ^ 3) for i in range(4)])]
    ppermute x1 -> x3, waiting for transfers between devices: 5.66 us -> 3.06 us  [the longest x1 2.11 us: per_device(): side = lax.ppermute(own, SIDE, [(0, 1), (1, 0)])]
    all_to_all x1, blocking collectives: 23.6 us -> 22 us  [per_device(): lax.all_to_all(stress, LAST, split_axis=0, concat_axis=0, tiled=True)]
    all_to_all x1, blocking collectives: 15.8 us -> 14.5 us  [per_device(): got = lax.all_to_all(sent, PAIR, split_axis=0, concat_axis=0, tiled=True)]
    all_to_all x1, waiting for transfers between devices: 0.65 us -> 0.01 us  [per_device(): lax.all_to_all(history, PLANE, split_axis=0, concat_axis=0, tiled=True)]
  transfers between devices with their start and end apart: 2 -> 4, of which waited for: 2 -> 2; matrix products, arithmetic and copies ran while one was open for 0% -> 0% of each run, Pallas kernels for 0% -> 1%
where the time goes in v8:
time: 61.1 us; the launch traced here: 60.4 us
  blocking collectives  36.5 us (60%)
  starting transfers between devices  17 us (28%)
  waiting for transfers between devices  3.06 us (5%)
  Pallas kernels  2.93 us (5%)
  other arithmetic  0.77 us (1%)
    all_to_all x1, blocking collectives, per_device(): lax.all_to_all(stress, LAST, split_axis=0, concat_axis=0, tiled=True)  22 us
    all_to_all x1, blocking collectives, per_device(): got = lax.all_to_all(sent, PAIR, split_axis=0, concat_axis=0, tiled=True)  14.5 us
    all_to_all x1, starting transfers between devices, per_device(): lax.all_to_all(history, PLANE, split_axis=0, concat_axis=0, tiled=True)  8.5 us
    ppermute x1, starting transfers between devices, per_device(): both = lax.ppermute(own, (SIDE, 'c'), [(i, i ^ 3) for i in range(4)])  4.24 us
    pallas_call x5, Pallas kernels, call(): pl.pallas_call(kernel, out_shape=shapes, in_specs=[pl.BlockSpec(memory_sp...  2.93 us
    ppermute x1, starting transfers between devices, per_device(): core = lax.ppermute(own, 'c', [(0, 1), (1, 0)])  2.15 us
    ppermute x1, waiting for transfers between devices, per_device(): side = lax.ppermute(own, SIDE, [(0, 1), (1, 0)])  2.11 us
    ppermute x1, starting transfers between devices, per_device(): side = lax.ppermute(own, SIDE, [(0, 1), (1, 0)])  2.08 us
  transfers between devices with their start and end apart: 4, of which 2 were waited for; matrix products, arithmetic and copies ran while one was open for 0% of the time, Pallas kernels for 1%

profile of v8, /device:TPU:1, one launch (start us, length us, event | category | flops | bytes accessed | tf_op | source)
XLA Modules:
  0.0 60.4 jit_solution(10836773087799904507)
XLA Ops:
  0.0 0.8 %pad_maximum_fusion.both_ref = f32[32,320]{1,0:T(8,128)S(1)} fusion(f32[32,192]{1,0:T(8,128)} %param.6, f32[32,128]{1,0:T(8,128)} %bitcast.6), kind=kLoop, calls=%fused_computation | loop fusion | flops 10240 | bytes 81920 | tf_op jit(solution)/shard_map/concatenate | solution.py:251
  0.8 0.2 shard_map.55
  1.0 14.5 %all_to_all.15.got_ref = f32[8,28,128]{2,1,0:T(8,128)S(1)} all-to-all(f32[8,28,128]{2,1,0:T(8,128)S(1)} %shard_map.55), channel_id=1, replica_groups=mesh['z2'=2,'z1'=2,'z0'=2,'y1'=2,'y0'=2,'x1'=2,'x0'=2,'y2'=2,'c'=2] {'x1..., dimensions={0} | all-to-all | bytes 229376 | tf_op jit(solution)/shard_map/all_to_all | solution.py:254
  15.5 0.8 %shard_map.57 = f32[16,16,256]{2,1,0:T(8,128)} custom-call(f32[8,28,128]{2,1,0:T(8,128)S(1)} %all_to_all.15.got_ref), custom_call_target="tpu_custom_call" | custom-call | bytes 114688 | tf_op jit(solution)/shard_map/pallas_call | solution.py:229
  16.3 8.5 %all-to-all-start.1 = ((f32[16,16,256]{2,1,0:T(8,128)}), f32[16,16,256]{2,1,0:T(8,128)S(1)}, u32[]{:S(2)}, u32[]{:S(2)}) async-start(f32[16,16,256]{2,1,0:T(8,128)} %shard_map.57), calls=%async_computation.1 | async-start | bytes 524288 | tf_op jit(solution)/shard_map/all_to_all | solution.py:256
  24.8 4.2 %collective-permute-start.2 = (f32[8,24,128]{2,1,0:T(8,128)S(1)}, f32[8,24,128]{2,1,0:T(8,128)S(1)}, u32[]{:S(2)}, u32[]{:S(2)}) collective-permute-start(f32[8,24,128]{2,1,0:T(8,128)S(1)} %slice.4.own_ref), channel_id=1, source_target_pairs={{0,17},{1,16},{16,1},{17,0},{2,19},{3,18},{18,3},{19,2},{4,21},{5,... | collective-permute-start | bytes 294920 | tf_op jit(solution)/shard_map/ppermute | solution.py:260
  29.1 2.1 %collective-permute-start.1 = (f32[8,24,128]{2,1,0:T(8,128)S(1)}, f32[8,24,128]{2,1,0:T(8,128)S(1)}, u32[]{:S(2)}, u32[]{:S(2)}) collective-permute-start(f32[8,24,128]{2,1,0:T(8,128)S(1)} %slice.4.own_ref), channel_id=1, source_target_pairs={{0,16},{16,0},{1,17},{17,1},{2,18},{18,2},{3,19},{19,3},{4,20},{20... | collective-permute-start | bytes 294920 | tf_op jit(solution)/shard_map/ppermute | solution.py:259
  31.2 2.1 %collective-permute-start = (f32[8,24,128]{2,1,0:T(8,128)S(1)}, f32[8,24,128]{2,1,0:T(8,128)S(1)}, u32[]{:S(2)}, u32[]{:S(2)}) collective-permute-start(f32[8,24,128]{2,1,0:T(8,128)S(1)} %slice.4.own_ref), channel_id=1, source_target_pairs={{0,1},{1,0},{2,3},{3,2},{4,5},{5,4},{6,7},{7,6},{8,9},{9,8},{10,11... | collective-permute-start | bytes 294920 | tf_op jit(solution)/shard_map/ppermute | solution.py:258
  33.3 1.0 %collective-permute-done.2.both_ref = f32[8,24,128]{2,1,0:T(8,128)S(1)} collective-permute-done((f32[8,24,128]{2,1,0:T(8,128)S(1)}, f32[8,24,128]{2,1,0:T(8,128)S(1)}, u32[]{:S(2)}, u32[]{:S(2)}) %collective-permute-start.2) | collective-permute-done | bytes 98336 | tf_op jit(solution)/shard_map/ppermute | solution.py:260
  34.3 2.1 %collective-permute-done.1.side_ref = f32[8,24,128]{2,1,0:T(8,128)S(1)} collective-permute-done((f32[8,24,128]{2,1,0:T(8,128)S(1)}, f32[8,24,128]{2,1,0:T(8,128)S(1)}, u32[]{:S(2)}, u32[]{:S(2)}) %collective-permute-start.1) | collective-permute-done | bytes 98336 | tf_op jit(solution)/shard_map/ppermute | solution.py:259
  36.4 0.0 collective-permute-done.core_ref
  36.4 0.3 shard_map.56
  36.7 0.0 all-to-all-done.1.steps_ref
  36.7 0.3 shard_map.58
  37.1 0.0 copy-start
  37.1 0.0 copy-start.1
  37.1 0.0 copy-start.2
  37.1 22.0 %all_to_all.16.got_ref = f32[32,24,128]{2,1,0:T(8,128)S(1)} all-to-all(f32[32,24,128]{2,1,0:T(8,128)S(1)} %shard_map.58), channel_id=1, replica_groups=mesh['z2'=2,'z1'=2,'z0'=2,'y1'=2,'y0'=2,'x1'=2,'x0'=2,'y2'=2,'c'=2] {'y2..., dimensions={0} | all-to-all | bytes 786432 | tf_op jit(solution)/shard_map/all_to_all | solution.py:277
  59.1 0.0 copy-done
  59.1 0.0 copy-done.1
  59.1 0.0 copy-done.2
  59.2 1.2 %shard_map.59 = f32[384,128]{1,0:T(8,128)} custom-call(f32[32,24,128]{2,1,0:T(8,128)S(1)} %all_to_all.16.got_ref, bf16[256,512]{1,0:T(8,128)(2,1)S(1)} %copy-done.1, bf16[256,512]{1,0:T(8,128)(2,1)S(1)} %copy-done, f32[2,16,256]{2,1,0:T(8,128)S(1)} %copy-done.2), custom_call_target="tpu_custom_call" | custom-call | bytes 950272 | tf_op jit(solution)/shard_map/pallas_call | solution.py:229
  (1 shorter events, 0.0 us)
Async XLA Ops:
  16.3 20.4 %all-to-all-start.1 = ((f32[16,16,256]{2,1,0:T(8,128)}), f32[16,16,256]{2,1,0:T(8,128)S(1)}, u32[]{:S(2)}, u32[]{:S(2)}) async-start(f32[16,16,256]{2,1,0:T(8,128)} %shard_map.57), calls=%async_computation.1 | async-start | bytes 524288 | tf_op jit(solution)/shard_map/all_to_all | solution.py:256
  24.8 9.4 %collective-permute-start.2 = (f32[8,24,128]{2,1,0:T(8,128)S(1)}, f32[8,24,128]{2,1,0:T(8,128)S(1)}, u32[]{:S(2)}, u32[]{:S(2)}) collective-permute-start(f32[8,24,128]{2,1,0:T(8,128)S(1)} %slice.4.own_ref), channel_id=1, source_target_pairs={{0,17},{1,16},{16,1},{17,0},{2,19},{3,18},{18,3},{19,2},{4,21},{5,... | collective-permute-start | bytes 294920 | tf_op jit(solution)/shard_map/ppermute | solution.py:260
  29.1 7.3 %collective-permute-start.1 = (f32[8,24,128]{2,1,0:T(8,128)S(1)}, f32[8,24,128]{2,1,0:T(8,128)S(1)}, u32[]{:S(2)}, u32[]{:S(2)}) collective-permute-start(f32[8,24,128]{2,1,0:T(8,128)S(1)} %slice.4.own_ref), channel_id=1, source_target_pairs={{0,16},{16,0},{1,17},{17,1},{2,18},{18,2},{3,19},{19,3},{4,20},{20... | collective-permute-start | bytes 294920 | tf_op jit(solution)/shard_map/ppermute | solution.py:259
  31.2 5.2 %collective-permute-start = (f32[8,24,128]{2,1,0:T(8,128)S(1)}, f32[8,24,128]{2,1,0:T(8,128)S(1)}, u32[]{:S(2)}, u32[]{:S(2)}) collective-permute-start(f32[8,24,128]{2,1,0:T(8,128)S(1)} %slice.4.own_ref), channel_id=1, source_target_pairs={{0,1},{1,0},{2,3},{3,2},{4,5},{5,4},{6,7},{7,6},{8,9},{9,8},{10,11... | collective-permute-start | bytes 294920 | tf_op jit(solution)/shard_map/ppermute | solution.py:258
  37.1 22.1 %copy-start = (bf16[256,512]{1,0:T(8,128)(2,1)S(1)}, bf16[256,512]{1,0:T(8,128)(2,1)}, u32[]{:S(2)}) copy-start(bf16[256,512]{1,0:T(8,128)(2,1)} %constant.7.clone.low_ref) | copy-start | bytes 786436
  37.1 22.0 %copy-start.1 = (bf16[256,512]{1,0:T(8,128)(2,1)S(1)}, bf16[256,512]{1,0:T(8,128)(2,1)}, u32[]{:S(2)}) copy-start(bf16[256,512]{1,0:T(8,128)(2,1)} %constant.6.clone.high_ref) | copy-start | bytes 786436
  37.1 22.0 %copy-start.2 = (f32[2,16,256]{2,1,0:T(8,128)S(1)}, f32[2,16,256]{2,1,0:T(8,128)}, u32[]{:S(2)}) copy-start(f32[2,16,256]{2,1,0:T(8,128)} %constant.8.clone.twist_ref) | copy-start | bytes 98308

commit v9 on v8

--- a/solution.py
+++ b/solution.py
@@ -14,11 +14,11 @@
 PAIR = ("x1", "x0", "c")
 PLANE = ("y1", "z2", "z1", "z0")
 SIDE = "y0"
-LAST = ("y2", "y0", "c", "x1", "x0")
+LAST = ("y2", "c", "y0", "x1", "x0")
 BLOCKS, SHARES, PAIRS = 16, 16, 8
 STEPS, MODES = 4096, 256
 SLOW, FAST = 256, 16
-OWNED, PADDED = 12, 16
+OWNED = 12
 LANES = 128
 f32, bf16 = jnp.float32, jnp.bfloat16
 NN = (((1,), (0,)), ((), ()))
@@ -31,9 +31,7 @@
 
 
 def product(a, b, dims):
-    (ah, al), (bh, bl) = a, b
-    dot = lambda x, y: lax.dot_general(x, y, dims, preferred_element_type=f32)
-    return dot(ah, bh) + (dot(ah, bl) + dot(al, bh))
+    return lax.dot_general(a, b, dims, preferred_element_type=f32)
 
 
 def tables():
@@ -49,7 +47,7 @@
     low = (first - high.astype(np.float64)).astype(jnp.bfloat16)
     turn = 2.0 * np.pi * (np.arange(FAST)[:, None] * k1[None, :]) / STEPS
     twist = np.stack([np.cos(turn), -np.sin(turn)])
-    return high, low, twist.astype(np.float32)
+    return np.concatenate([high, low, high]), twist.astype(np.float32)
 
 
 def scatter(both_ref, out_ref, wide, tall):
@@ -95,7 +93,7 @@
         out_ref[:, :, lanes] = jnp.broadcast_to(joined, (BLOCKS,) + joined.shape)
 
 
-def order_modes(own_ref, core_ref, side_ref, both_ref, high_ref, low_ref, whole):
+def order_modes(own_ref, core_ref, side_ref, both_ref, out_ref, whole):
     side, core = lax.axis_index(SIDE), lax.axis_index("c")
     modes = MODES // PAIRS
     half = modes // 2
@@ -114,8 +112,10 @@
                     whole[rows, LANES:] = ref[
                         sender, pl.ds(half, half // 2), pl.ds(part * rest, rest)
                     ]
-        to = (pl.ds(pl.multiple_of(which * width, width), width), slice(None))
-        high_ref[to], low_ref[to] = split(whole[...].T)
+        to = pl.ds(pl.multiple_of(which * width, width), width)
+        high, low = split(whole[...].T)
+        for part, value in enumerate((high, high, low)):
+            out_ref[to, pl.ds(part * MODES, MODES)] = value
 
 
 def index_of(axes, **at):
@@ -131,13 +131,13 @@
     return [dict(zip(axes, map(int, column))) for column in grid.T]
 
 
-def contract(high_ref, low_ref, steps_ref, out_ref):
+def contract(modes_ref, steps_ref, out_ref):
     steps = [
         steps_ref[:, pl.ds(8 * high, 8), :].reshape(LANES, MODES) for high in range(2)
     ]
-    stress = product(
-        (high_ref[...], low_ref[...]), split(jnp.concatenate(steps)), NT
-    )
+    high, low = split(jnp.concatenate(steps))
+    parts = jnp.concatenate([high, low, high], axis=1)
+    stress = product(modes_ref[...], parts, NT)
     for side in range(2):
         for share in range(SHARES):
             owner = index_of(LAST, **{SIDE: side}, **places(MODE)[share])
@@ -185,27 +185,30 @@
     return low + high
 
 
-def spectra(got_ref, high_ref, low_ref, twist_ref, out_ref, rows_high, rows_low, stage):
+def spectra(got_ref, first_ref, twist_ref, out_hbm, rows, stage, result, sems):
+    tops = ((0, 8, 0), (8, OWNED - 8, 8 * FAST))
     for n2 in range(FAST):
         for side in range(2):
-            at = (pl.ds(n2 * PADDED, OWNED), pl.ds(side * LANES, LANES))
-            rows = pl.ds(n2 // 8 * OWNED, OWNED)
+            part = pl.ds(n2 // 8 * OWNED, OWNED)
             place = places(PAIR)[n2 % 8]
             senders = [index_of(LAST, **{SIDE: side}, y2=y2, **place) for y2 in range(2)]
-            value = got_ref[senders[0], rows, :] + got_ref[senders[1], rows, :]
-            rows_high[at], rows_low[at] = split(value)
-    stage[...] = product(
-        (rows_high[...], rows_low[...]), (high_ref[...], low_ref[...]), NN
-    )
+            value = got_ref[senders[0], part, :] + got_ref[senders[1], part, :]
+            for top, count, base in tops:
+                at = (pl.ds(base + n2 * count, count), pl.ds(side * LANES, LANES))
+                rows[at] = value[top : top + count]
+    high, low = split(rows[...])
+    parts = jnp.concatenate([high, high, low], axis=1)
+    stage[...] = product(parts, first_ref[...], NN)
     tiles = STEPS // 2 // LANES
-    for top in range(0, OWNED, 8):
+    copies = []
+    for top, count, base in tops:
         for left in range(0, SLOW, LANES):
             values = []
             for n2 in range(FAST):
-                rows = pl.ds(n2 * PADDED + top, 8)
+                at = pl.ds(base + n2 * count, count)
                 value = (
-                    stage[rows, pl.ds(left, LANES)],
-                    stage[rows, pl.ds(SLOW + left, LANES)],
+                    stage[at, pl.ds(left, LANES)],
+                    stage[at, pl.ds(SLOW + left, LANES)],
                 )
                 if n2:
                     lanes = pl.ds(left, LANES)
@@ -215,17 +218,23 @@
                         twist_ref[1, pl.ds(n2, 1), lanes],
                     )
                 values.append(value)
-            valid = min(8, OWNED - top)
             for k2, value in enumerate(transform(values)[: FAST // 2]):
                 tile = (k2 * SLOW + left) // LANES
                 for part in range(2):
                     first = (top * tiles + tile) * 2 + part
-                    to = pl.ds(first, valid, stride=2 * tiles)
-                    out_ref[to, :] = value[part][:valid]
-
-
-def call(kernel, shapes, *args, scratch=(), space=pltpu.VMEM, limit=8 << 20):
-    whole = pl.BlockSpec(memory_space=pltpu.VMEM)
+                    result[pl.ds(first, count, stride=2 * tiles), :] = value[part]
+        done = pl.ds(top * 2 * tiles, count * 2 * tiles)
+        copy = pltpu.make_async_copy(
+            result.at[done, :], out_hbm.at[done, :], sems.at[len(copies)]
+        )
+        copy.start()
+        copies.append(copy)
+    for copy in copies:
+        copy.wait()
+
+
+def call(kernel, shapes, *args, scratch=(), space=pltpu.VMEM, out=pltpu.VMEM, limit=8 << 20):
+    whole = pl.BlockSpec(memory_space=out)
     return pl.pallas_call(
         kernel,
         out_shape=shapes,
@@ -258,9 +267,9 @@
     core = lax.ppermute(own, "c", [(0, 1), (1, 0)])
     side = lax.ppermute(own, SIDE, [(0, 1), (1, 0)])
     both = lax.ppermute(own, (SIDE, "c"), [(i, i ^ 3) for i in range(4)])
-    high, low = call(
+    ordered = call(
         order_modes,
-        (shape((2 * width, MODES), bf16), shape((2 * width, MODES), bf16)),
+        shape((2 * width, 3 * MODES), bf16),
         own,
         core,
         side,
@@ -270,21 +279,21 @@
     stress = call(
         contract,
         shape((2 * SHARES, 2 * OWNED, LANES), f32),
-        high,
-        low,
+        ordered,
         steps,
     )
     owned = lax.all_to_all(stress, LAST, split_axis=0, concat_axis=0, tiled=True)
-    first_high, first_low, twist = tables()
-    rows = FAST * PADDED
+    first, twist = tables()
+    rows = FAST * OWNED
     out = call(
         spectra,
         shape((OWNED * STEPS // LANES, LANES), f32),
         owned,
-        first_high,
-        first_low,
+        first,
         twist,
-        scratch=[vmem((rows, SLOW), bf16)] * 2 + [vmem((rows, 2 * SLOW), f32)],
+        scratch=[vmem((rows, SLOW), f32), vmem((rows, 2 * SLOW), f32)]
+        + [vmem((OWNED * STEPS // LANES, LANES), f32), pltpu.SemaphoreType.DMA((2,))],
+        out=pltpu.HBM,
     )
     out = out.reshape(OWNED, STEPS // 2 // LANES, 2, LANES).transpose(0, 2, 1, 3)
     return out.reshape(OWNED, 2, STEPS // 2)

time: 61.1 us -> 60.9 us (level)
  no operation moved by 1% of the time
where the time goes in v9:
time: 60.9 us; the launch traced here: 60.4 us
  blocking collectives  36.7 us (60%)
  starting transfers between devices  17 us (28%)
  waiting for transfers between devices  3.06 us (5%)
  Pallas kernels  2.87 us (5%)
  other arithmetic  0.77 us (1%)
    all_to_all x1, blocking collectives, per_device(): lax.all_to_all(stress, LAST, split_axis=0, concat_axis=0, tiled=True)  22.1 us
    all_to_all x1, blocking collectives, per_device(): got = lax.all_to_all(sent, PAIR, split_axis=0, concat_axis=0, tiled=True)  14.5 us
    all_to_all x1, starting transfers between devices, per_device(): lax.all_to_all(history, PLANE, split_axis=0, concat_axis=0, tiled=True)  8.5 us
    ppermute x1, starting transfers between devices, per_device(): both = lax.ppermute(own, (SIDE, 'c'), [(i, i ^ 3) for i in range(4)])  4.24 us
    pallas_call x5, Pallas kernels, call(): pl.pallas_call(kernel, out_shape=shapes, in_specs=[pl.BlockSpec(memory_sp...  2.87 us
    ppermute x1, starting transfers between devices, per_device(): core = lax.ppermute(own, 'c', [(0, 1), (1, 0)])  2.15 us
    ppermute x1, waiting for transfers between devices, per_device(): side = lax.ppermute(own, SIDE, [(0, 1), (1, 0)])  2.11 us
    ppermute x1, starting transfers between devices, per_device(): side = lax.ppermute(own, SIDE, [(0, 1), (1, 0)])  2.08 us
  transfers between devices with their start and end apart: 4, of which 2 were waited for; matrix products, arithmetic and copies ran while one was open for 0% of the time, Pallas kernels for 1%

profile of v9, /device:TPU:1, one launch (start us, length us, event | category | flops | bytes accessed | tf_op | source)
XLA Modules:
  0.0 60.4 jit_solution(1694657175281001969)
XLA Ops:
  0.0 0.8 %pad_maximum_fusion.both_ref = f32[32,320]{1,0:T(8,128)S(1)} fusion(f32[32,192]{1,0:T(8,128)} %param.5, f32[32,128]{1,0:T(8,128)} %bitcast.6), kind=kLoop, calls=%fused_computation | loop fusion | flops 10240 | bytes 81920 | tf_op jit(solution)/shard_map/concatenate | solution.py:260
  0.8 0.2 shard_map.46
  1.0 14.5 %all_to_all.15.got_ref = f32[8,28,128]{2,1,0:T(8,128)S(1)} all-to-all(f32[8,28,128]{2,1,0:T(8,128)S(1)} %shard_map.46), channel_id=1, replica_groups=mesh['z2'=2,'z1'=2,'z0'=2,'y1'=2,'y0'=2,'x1'=2,'x0'=2,'y2'=2,'c'=2] {'x1..., dimensions={0} | all-to-all | bytes 229376 | tf_op jit(solution)/shard_map/all_to_all | solution.py:263
  15.5 0.8 %shard_map.48 = f32[16,16,256]{2,1,0:T(8,128)} custom-call(f32[8,28,128]{2,1,0:T(8,128)S(1)} %all_to_all.15.got_ref), custom_call_target="tpu_custom_call" | custom-call | bytes 114688 | tf_op jit(solution)/shard_map/pallas_call | solution.py:238
  16.3 8.5 %all-to-all-start.1 = ((f32[16,16,256]{2,1,0:T(8,128)}), f32[16,16,256]{2,1,0:T(8,128)S(1)}, u32[]{:S(2)}, u32[]{:S(2)}) async-start(f32[16,16,256]{2,1,0:T(8,128)} %shard_map.48), calls=%async_computation.1 | async-start | bytes 524288 | tf_op jit(solution)/shard_map/all_to_all | solution.py:265
  24.9 4.2 %collective-permute-start.2 = (f32[8,24,128]{2,1,0:T(8,128)S(1)}, f32[8,24,128]{2,1,0:T(8,128)S(1)}, u32[]{:S(2)}, u32[]{:S(2)}) collective-permute-start(f32[8,24,128]{2,1,0:T(8,128)S(1)} %slice.4.own_ref), channel_id=1, source_target_pairs={{0,17},{1,16},{16,1},{17,0},{2,19},{3,18},{18,3},{19,2},{4,21},{5,... | collective-permute-start | bytes 294920 | tf_op jit(solution)/shard_map/ppermute | solution.py:269
  29.1 2.1 %collective-permute-start.1 = (f32[8,24,128]{2,1,0:T(8,128)S(1)}, f32[8,24,128]{2,1,0:T(8,128)S(1)}, u32[]{:S(2)}, u32[]{:S(2)}) collective-permute-start(f32[8,24,128]{2,1,0:T(8,128)S(1)} %slice.4.own_ref), channel_id=1, source_target_pairs={{0,16},{16,0},{1,17},{17,1},{2,18},{18,2},{3,19},{19,3},{4,20},{20... | collective-permute-start | bytes 294920 | tf_op jit(solution)/shard_map/ppermute | solution.py:268
  31.2 2.1 %collective-permute-start = (f32[8,24,128]{2,1,0:T(8,128)S(1)}, f32[8,24,128]{2,1,0:T(8,128)S(1)}, u32[]{:S(2)}, u32[]{:S(2)}) collective-permute-start(f32[8,24,128]{2,1,0:T(8,128)S(1)} %slice.4.own_ref), channel_id=1, source_target_pairs={{0,1},{1,0},{2,3},{3,2},{4,5},{5,4},{6,7},{7,6},{8,9},{9,8},{10,11... | collective-permute-start | bytes 294920 | tf_op jit(solution)/shard_map/ppermute | solution.py:267
  33.3 1.0 %collective-permute-done.2.both_ref = f32[8,24,128]{2,1,0:T(8,128)S(1)} collective-permute-done((f32[8,24,128]{2,1,0:T(8,128)S(1)}, f32[8,24,128]{2,1,0:T(8,128)S(1)}, u32[]{:S(2)}, u32[]{:S(2)}) %collective-permute-start.2) | collective-permute-done | bytes 98336 | tf_op jit(solution)/shard_map/ppermute | solution.py:269
  34.3 2.1 %collective-permute-done.1.side_ref = f32[8,24,128]{2,1,0:T(8,128)S(1)} collective-permute-done((f32[8,24,128]{2,1,0:T(8,128)S(1)}, f32[8,24,128]{2,1,0:T(8,128)S(1)}, u32[]{:S(2)}, u32[]{:S(2)}) %collective-permute-start.1) | collective-permute-done | bytes 98336 | tf_op jit(solution)/shard_map/ppermute | solution.py:268
  36.4 0.0 collective-permute-done.core_ref
  36.4 0.3 shard_map.47.modes_ref
  36.7 0.0 copy-start
  36.7 0.0 all-to-all-done.1.steps_ref
  36.8 0.4 shard_map.49
  37.1 0.0 copy-start.1
  37.1 22.1 %all_to_all.16.got_ref = f32[32,24,128]{2,1,0:T(8,128)S(1)} all-to-all(f32[32,24,128]{2,1,0:T(8,128)S(1)} %shard_map.49), channel_id=1, replica_groups=mesh['z2'=2,'z1'=2,'z0'=2,'y1'=2,'y0'=2,'x1'=2,'x0'=2,'y2'=2,'c'=2] {'y2..., dimensions={0} | all-to-all | bytes 786432 | tf_op jit(solution)/shard_map/all_to_all | solution.py:285
  59.3 0.0 copy-done
  59.3 0.0 copy-done.1
  59.3 1.2 %shard_map.50 = f32[384,128]{1,0:T(8,128)} custom-call(f32[32,24,128]{2,1,0:T(8,128)S(1)} %all_to_all.16.got_ref, bf16[768,512]{1,0:T(8,128)(2,1)S(1)} %copy-done, f32[2,16,256]{2,1,0:T(8,128)S(1)} %copy-done.1), custom_call_target="tpu_custom_call" | custom-call | bytes 1212416 | tf_op jit(solution)/shard_map/pallas_call | solution.py:238
  (1 shorter events, 0.0 us)
Async XLA Ops:
  16.3 20.4 %all-to-all-start.1 = ((f32[16,16,256]{2,1,0:T(8,128)}), f32[16,16,256]{2,1,0:T(8,128)S(1)}, u32[]{:S(2)}, u32[]{:S(2)}) async-start(f32[16,16,256]{2,1,0:T(8,128)} %shard_map.48), calls=%async_computation.1 | async-start | bytes 524288 | tf_op jit(solution)/shard_map/all_to_all | solution.py:265
  24.9 9.4 %collective-permute-start.2 = (f32[8,24,128]{2,1,0:T(8,128)S(1)}, f32[8,24,128]{2,1,0:T(8,128)S(1)}, u32[]{:S(2)}, u32[]{:S(2)}) collective-permute-start(f32[8,24,128]{2,1,0:T(8,128)S(1)} %slice.4.own_ref), channel_id=1, source_target_pairs={{0,17},{1,16},{16,1},{17,0},{2,19},{3,18},{18,3},{19,2},{4,21},{5,... | collective-permute-start | bytes 294920 | tf_op jit(solution)/shard_map/ppermute | solution.py:269
  29.1 7.3 %collective-permute-start.1 = (f32[8,24,128]{2,1,0:T(8,128)S(1)}, f32[8,24,128]{2,1,0:T(8,128)S(1)}, u32[]{:S(2)}, u32[]{:S(2)}) collective-permute-start(f32[8,24,128]{2,1,0:T(8,128)S(1)} %slice.4.own_ref), channel_id=1, source_target_pairs={{0,16},{16,0},{1,17},{17,1},{2,18},{18,2},{3,19},{19,3},{4,20},{20... | collective-permute-start | bytes 294920 | tf_op jit(solution)/shard_map/ppermute | solution.py:268
  31.2 5.2 %collective-permute-start = (f32[8,24,128]{2,1,0:T(8,128)S(1)}, f32[8,24,128]{2,1,0:T(8,128)S(1)}, u32[]{:S(2)}, u32[]{:S(2)}) collective-permute-start(f32[8,24,128]{2,1,0:T(8,128)S(1)} %slice.4.own_ref), channel_id=1, source_target_pairs={{0,1},{1,0},{2,3},{3,2},{4,5},{5,4},{6,7},{7,6},{8,9},{9,8},{10,11... | collective-permute-start | bytes 294920 | tf_op jit(solution)/shard_map/ppermute | solution.py:267
  36.7 22.5 %copy-start = (bf16[768,512]{1,0:T(8,128)(2,1)S(1)}, bf16[768,512]{1,0:T(8,128)(2,1)}, u32[]{:S(2)}) copy-start(bf16[768,512]{1,0:T(8,128)(2,1)} %constant.4.clone.first_ref) | copy-start | bytes 2359300
  37.1 22.1 %copy-start.1 = (f32[2,16,256]{2,1,0:T(8,128)S(1)}, f32[2,16,256]{2,1,0:T(8,128)}, u32[]{:S(2)}) copy-start(f32[2,16,256]{2,1,0:T(8,128)} %constant.5.clone.twist_ref) | copy-start | bytes 98308

commit v10 on v9

--- a/solution.py
+++ b/solution.py
@@ -265,8 +265,8 @@
     steps = lax.all_to_all(history, PLANE, split_axis=0, concat_axis=0, tiled=True)
     own = got[:, :24]
     core = lax.ppermute(own, "c", [(0, 1), (1, 0)])
+    both = lax.ppermute(own, (SIDE, "c"), [(i, i ^ 3) for i in range(4)])
     side = lax.ppermute(own, SIDE, [(0, 1), (1, 0)])
-    both = lax.ppermute(own, (SIDE, "c"), [(i, i ^ 3) for i in range(4)])
     ordered = call(
         order_modes,
         shape((2 * width, 3 * MODES), bf16),

time: 60.9 us -> 60.9 us (level)
  no operation moved by 1% of the time
where the time goes in v10:
time: 60.9 us; the launch traced here: 60.4 us
  blocking collectives  36.7 us (60%)
  starting transfers between devices  17 us (28%)
  waiting for transfers between devices  3.06 us (5%)
  Pallas kernels  2.87 us (5%)
  other arithmetic  0.77 us (1%)
    all_to_all x1, blocking collectives, per_device(): lax.all_to_all(stress, LAST, split_axis=0, concat_axis=0, tiled=True)  22.1 us
    all_to_all x1, blocking collectives, per_device(): got = lax.all_to_all(sent, PAIR, split_axis=0, concat_axis=0, tiled=True)  14.5 us
    all_to_all x1, starting transfers between devices, per_device(): lax.all_to_all(history, PLANE, split_axis=0, concat_axis=0, tiled=True)  8.5 us
    ppermute x1, starting transfers between devices, per_device(): both = lax.ppermute(own, (SIDE, 'c'), [(i, i ^ 3) for i in range(4)])  4.24 us
    pallas_call x5, Pallas kernels, call(): pl.pallas_call(kernel, out_shape=shapes, in_specs=[pl.BlockSpec(memory_sp...  2.87 us
    ppermute x1, starting transfers between devices, per_device(): core = lax.ppermute(own, 'c', [(0, 1), (1, 0)])  2.15 us
    ppermute x1, waiting for transfers between devices, per_device(): side = lax.ppermute(own, SIDE, [(0, 1), (1, 0)])  2.11 us
    ppermute x1, starting transfers between devices, per_device(): side = lax.ppermute(own, SIDE, [(0, 1), (1, 0)])  2.08 us
  transfers between devices with their start and end apart: 4, of which 2 were waited for; matrix products, arithmetic and copies ran while one was open for 0% of the time, Pallas kernels for 1%

profile of v10, /device:TPU:1, one launch (start us, length us, event | category | flops | bytes accessed | tf_op | source)
XLA Modules:
  0.0 60.4 jit_solution(1694657175281001969)
XLA Ops:
  0.0 0.8 %pad_maximum_fusion.both_ref = f32[32,320]{1,0:T(8,128)S(1)} fusion(f32[32,192]{1,0:T(8,128)} %param.5, f32[32,128]{1,0:T(8,128)} %bitcast.6), kind=kLoop, calls=%fused_computation | loop fusion | flops 10240 | bytes 81920 | tf_op jit(solution)/shard_map/concatenate | solution.py:260
  0.8 0.2 shard_map.46
  1.0 14.5 %all_to_all.15.got_ref = f32[8,28,128]{2,1,0:T(8,128)S(1)} all-to-all(f32[8,28,128]{2,1,0:T(8,128)S(1)} %shard_map.46), channel_id=1, replica_groups=mesh['z2'=2,'z1'=2,'z0'=2,'y1'=2,'y0'=2,'x1'=2,'x0'=2,'y2'=2,'c'=2] {'x1..., dimensions={0} | all-to-all | bytes 229376 | tf_op jit(solution)/shard_map/all_to_all | solution.py:263
  15.5 0.8 %shard_map.48 = f32[16,16,256]{2,1,0:T(8,128)} custom-call(f32[8,28,128]{2,1,0:T(8,128)S(1)} %all_to_all.15.got_ref), custom_call_target="tpu_custom_call" | custom-call | bytes 114688 | tf_op jit(solution)/shard_map/pallas_call | solution.py:238
  16.3 8.5 %all-to-all-start.1 = ((f32[16,16,256]{2,1,0:T(8,128)}), f32[16,16,256]{2,1,0:T(8,128)S(1)}, u32[]{:S(2)}, u32[]{:S(2)}) async-start(f32[16,16,256]{2,1,0:T(8,128)} %shard_map.48), calls=%async_computation.1 | async-start | bytes 524288 | tf_op jit(solution)/shard_map/all_to_all | solution.py:265
  24.9 4.2 %collective-permute-start.2 = (f32[8,24,128]{2,1,0:T(8,128)S(1)}, f32[8,24,128]{2,1,0:T(8,128)S(1)}, u32[]{:S(2)}, u32[]{:S(2)}) collective-permute-start(f32[8,24,128]{2,1,0:T(8,128)S(1)} %slice.4.own_ref), channel_id=1, source_target_pairs={{0,17},{1,16},{16,1},{17,0},{2,19},{3,18},{18,3},{19,2},{4,21},{5,... | collective-permute-start | bytes 294920 | tf_op jit(solution)/shard_map/ppermute | solution.py:268
  29.1 2.1 %collective-permute-start.1 = (f32[8,24,128]{2,1,0:T(8,128)S(1)}, f32[8,24,128]{2,1,0:T(8,128)S(1)}, u32[]{:S(2)}, u32[]{:S(2)}) collective-permute-start(f32[8,24,128]{2,1,0:T(8,128)S(1)} %slice.4.own_ref), channel_id=1, source_target_pairs={{0,16},{16,0},{1,17},{17,1},{2,18},{18,2},{3,19},{19,3},{4,20},{20... | collective-permute-start | bytes 294920 | tf_op jit(solution)/shard_map/ppermute | solution.py:269
  31.2 2.1 %collective-permute-start = (f32[8,24,128]{2,1,0:T(8,128)S(1)}, f32[8,24,128]{2,1,0:T(8,128)S(1)}, u32[]{:S(2)}, u32[]{:S(2)}) collective-permute-start(f32[8,24,128]{2,1,0:T(8,128)S(1)} %slice.4.own_ref), channel_id=1, source_target_pairs={{0,1},{1,0},{2,3},{3,2},{4,5},{5,4},{6,7},{7,6},{8,9},{9,8},{10,11... | collective-permute-start | bytes 294920 | tf_op jit(solution)/shard_map/ppermute | solution.py:267
  33.3 1.0 %collective-permute-done.2.both_ref = f32[8,24,128]{2,1,0:T(8,128)S(1)} collective-permute-done((f32[8,24,128]{2,1,0:T(8,128)S(1)}, f32[8,24,128]{2,1,0:T(8,128)S(1)}, u32[]{:S(2)}, u32[]{:S(2)}) %collective-permute-start.2) | collective-permute-done | bytes 98336 | tf_op jit(solution)/shard_map/ppermute | solution.py:268
  34.3 2.1 %collective-permute-done.1.side_ref = f32[8,24,128]{2,1,0:T(8,128)S(1)} collective-permute-done((f32[8,24,128]{2,1,0:T(8,128)S(1)}, f32[8,24,128]{2,1,0:T(8,128)S(1)}, u32[]{:S(2)}, u32[]{:S(2)}) %collective-permute-start.1) | collective-permute-done | bytes 98336 | tf_op jit(solution)/shard_map/ppermute | solution.py:269
  36.4 0.0 collective-permute-done.core_ref
  36.4 0.3 shard_map.47.modes_ref
  36.7 0.0 copy-start
  36.7 0.0 all-to-all-done.1.steps_ref
  36.8 0.4 shard_map.49
  37.1 0.0 copy-start.1
  37.1 22.1 %all_to_all.16.got_ref = f32[32,24,128]{2,1,0:T(8,128)S(1)} all-to-all(f32[32,24,128]{2,1,0:T(8,128)S(1)} %shard_map.49), channel_id=1, replica_groups=mesh['z2'=2,'z1'=2,'z0'=2,'y1'=2,'y0'=2,'x1'=2,'x0'=2,'y2'=2,'c'=2] {'y2..., dimensions={0} | all-to-all | bytes 786432 | tf_op jit(solution)/shard_map/all_to_all | solution.py:285
  59.3 0.0 copy-done
  59.3 0.0 copy-done.1
  59.3 1.2 %shard_map.50 = f32[384,128]{1,0:T(8,128)} custom-call(f32[32,24,128]{2,1,0:T(8,128)S(1)} %all_to_all.16.got_ref, bf16[768,512]{1,0:T(8,128)(2,1)S(1)} %copy-done, f32[2,16,256]{2,1,0:T(8,128)S(1)} %copy-done.1), custom_call_target="tpu_custom_call" | custom-call | bytes 1212416 | tf_op jit(solution)/shard_map/pallas_call | solution.py:238
  (1 shorter events, 0.0 us)
Async XLA Ops:
  16.3 20.4 %all-to-all-start.1 = ((f32[16,16,256]{2,1,0:T(8,128)}), f32[16,16,256]{2,1,0:T(8,128)S(1)}, u32[]{:S(2)}, u32[]{:S(2)}) async-start(f32[16,16,256]{2,1,0:T(8,128)} %shard_map.48), calls=%async_computation.1 | async-start | bytes 524288 | tf_op jit(solution)/shard_map/all_to_all | solution.py:265
  24.9 9.4 %collective-permute-start.2 = (f32[8,24,128]{2,1,0:T(8,128)S(1)}, f32[8,24,128]{2,1,0:T(8,128)S(1)}, u32[]{:S(2)}, u32[]{:S(2)}) collective-permute-start(f32[8,24,128]{2,1,0:T(8,128)S(1)} %slice.4.own_ref), channel_id=1, source_target_pairs={{0,17},{1,16},{16,1},{17,0},{2,19},{3,18},{18,3},{19,2},{4,21},{5,... | collective-permute-start | bytes 294920 | tf_op jit(solution)/shard_map/ppermute | solution.py:268
  29.1 7.3 %collective-permute-start.1 = (f32[8,24,128]{2,1,0:T(8,128)S(1)}, f32[8,24,128]{2,1,0:T(8,128)S(1)}, u32[]{:S(2)}, u32[]{:S(2)}) collective-permute-start(f32[8,24,128]{2,1,0:T(8,128)S(1)} %slice.4.own_ref), channel_id=1, source_target_pairs={{0,16},{16,0},{1,17},{17,1},{2,18},{18,2},{3,19},{19,3},{4,20},{20... | collective-permute-start | bytes 294920 | tf_op jit(solution)/shard_map/ppermute | solution.py:269
  31.2 5.2 %collective-permute-start = (f32[8,24,128]{2,1,0:T(8,128)S(1)}, f32[8,24,128]{2,1,0:T(8,128)S(1)}, u32[]{:S(2)}, u32[]{:S(2)}) collective-permute-start(f32[8,24,128]{2,1,0:T(8,128)S(1)} %slice.4.own_ref), channel_id=1, source_target_pairs={{0,1},{1,0},{2,3},{3,2},{4,5},{5,4},{6,7},{7,6},{8,9},{9,8},{10,11... | collective-permute-start | bytes 294920 | tf_op jit(solution)/shard_map/ppermute | solution.py:267
  36.7 22.5 %copy-start = (bf16[768,512]{1,0:T(8,128)(2,1)S(1)}, bf16[768,512]{1,0:T(8,128)(2,1)}, u32[]{:S(2)}) copy-start(bf16[768,512]{1,0:T(8,128)(2,1)} %constant.4.clone.first_ref) | copy-start | bytes 2359300
  37.1 22.1 %copy-start.1 = (f32[2,16,256]{2,1,0:T(8,128)S(1)}, f32[2,16,256]{2,1,0:T(8,128)}, u32[]{:S(2)}) copy-start(f32[2,16,256]{2,1,0:T(8,128)} %constant.5.clone.twist_ref) | copy-start | bytes 98308
